TPU v7x, 768 devices: a whole 4x8x12 slice. The times are simulated.
768 devices in a mesh: ctx: 32 (over x, y_hi, core), section: 24 (over y_lo, z).
Axes of the slice: x: 4, y: 8 (y_hi: 4, y_lo: 2; y = y_hi * 2 + y_lo), z: 12, core: 2. Of those that a mesh axis runs over, the one named last changes fastest.
Arguments:
- queries: bfloat16 [24, 4096, 4096], P('section', 'ctx'), may hold values from -24 to 24
- keys: bfloat16 [24, 4096, 512], P('section', 'ctx'), may hold values from -24 to 24
- values: bfloat16 [24, 4096, 512], P('section', 'ctx'), may hold values from -6 to 6
- doc_lengths: int32 [24, 4], P('section'), may hold values from 1 to 2048, 4096 in all within a row
- interp_num: int32 [1], replicated, may hold values from 250 to 999
- interp_den: int32 [1], replicated, may hold values from 1000 to 1999
Outputs:
- handed: bfloat16 [24, 4096, 4096], P('section', 'ctx')
Inputs may be any that keep to these rules, and one draw needn't show every extreme that they name: `doc_lengths`: each row sums to 4096; its longest document has exactly 2048 tokens.
All inputs are finite; a program needn't handle non-finite values.
Results may differ from a plain program's by a relative error of at most 0.0099.
Values may be sent and summed in bfloat16 or wider, within the bound.
No kernel may reach another device: no remote copies, remote signals or barrier semaphores. Data moves between devices by JAX's collectives and lax.ppermute only.
A program may use at most 64 MiB of HBM per device.

v0:
```python
import functools
import math

import jax
import jax.numpy as jnp
import numpy as np
from jax import lax
from jax.experimental import pallas as pl
from jax.experimental.pallas import tpu as pltpu
from jax.sharding import Mesh, PartitionSpec as P


KV_HEADS = 4
GROUP = 8
HEAD = 128
THETA = 500000.0
MASKED = -1e30
SPAN = 64
TOKENS = 4096
TILE = 512
ROUNDS = 2112 // TILE + 1
QUERY_SCALE = math.log2(math.e) / math.sqrt(HEAD)
AXES = ("x", "yh", "c", "yl", "z")
SIZES = (4, 4, 2, 2, 12)


def route(dx, ds):
    pairs = []
    for i in range(math.prod(SIZES)):
        x, yh, c, yl, z = (int(a) for a in np.unravel_index(i, SIZES))
        s = (yl * SIZES[4] + z + ds) % (SIZES[3] * SIZES[4])
        to = ((x + dx) % 4, yh, c, s // SIZES[4], s % SIZES[4])
        pairs.append((i, int(np.ravel_multi_index(to, SIZES))))
    return pairs


def frequencies():
    half = HEAD // 2
    freq = THETA ** (-(2.0 * np.arange(half)) / HEAD)
    return np.concatenate([freq, freq]).astype(np.float32)[None]


def doc_start(position, lens_ref):
    end = 0
    start = jnp.zeros_like(position)
    for d in range(4):
        length = lens_ref[0, d]
        end = end + length
        start = start + jnp.where(position >= end, length, 0)
    return start


def pack_kernel(where_ref, lens_ref, num_ref, den_ref, freq_ref, q_ref, k_ref, v_ref, kv_ref, *q_out):
    x = where_ref[0]
    shard = x * 8 + where_ref[1] * 2 + where_ref[2]
    row = lax.broadcasted_iota(jnp.int32, (128, HEAD), 0)
    lane = lax.broadcasted_iota(jnp.int32, (128, HEAD), 1)
    position = jnp.where(row < SPAN, shard * SPAN + row, (63 - shard) * SPAN + row - SPAN)
    offset = (position - doc_start(position, lens_ref)).astype(jnp.float32)
    ratio = jnp.full((128, HEAD), num_ref[0], jnp.int32).astype(jnp.float32) / jnp.full(
        (128, HEAD), den_ref[0], jnp.int32
    ).astype(jnp.float32)
    angle = offset * ratio * freq_ref[...]
    cosine = jnp.cos(angle)
    sine = jnp.sin(angle)
    sine = jnp.where(lane < HEAD // 2, -sine, sine)
    for h in range(KV_HEADS):
        cols = slice(h * HEAD, (h + 1) * HEAD)
        wide = k_ref[:, cols].astype(jnp.float32)
        turned = (wide * cosine + pltpu.roll(wide, HEAD // 2, 1) * sine).astype(jnp.bfloat16)
        kv_ref[h, :, :HEAD] = turned
        kv_ref[h, :, HEAD:] = v_ref[:, cols]
    cosine = cosine * QUERY_SCALE
    sine = sine * QUERY_SCALE
    for d in range(4):
        group = lax.rem(x + d, 4)
        for h in range(GROUP):
            start = pl.multiple_of(group * (GROUP * HEAD) + h * HEAD, HEAD)
            wide = q_ref[:, pl.ds(start, HEAD)].astype(jnp.float32)
            turned = wide * cosine + pltpu.roll(wide, HEAD // 2, 1) * sine
            q_out[d][:, h * HEAD : (h + 1) * HEAD] = turned.astype(jnp.bfloat16)


def gather_keys(where_ref, blocks, kv_ref):
    yh, core = where_ref[1], where_ref[2]
    sides = (0, 2 * core - 1, 1 - 2 * core, 2)
    for block, side in zip(blocks, sides):
        y = lax.rem(yh + side + 4, 4)
        for c in range(2):
            for x in range(4):
                shard = x * 8 + y * 2 + c
                early = pl.multiple_of(shard * SPAN, SPAN)
                late = pl.multiple_of((63 - shard) * SPAN, SPAN)
                kv_ref[pl.ds(early, SPAN), :] = block[c, x, :SPAN, :]
                kv_ref[pl.ds(late, SPAN), :] = block[c, x, SPAN:, :]
    kv_ref[TOKENS:, :] = jnp.zeros((TILE, 2 * HEAD), jnp.bfloat16)


def attend_block(where_ref, lens_ref, dx, q_ref, kv_ref, o_ref, s_scr, m_scr, acc_scr):
    shard = lax.rem(where_ref[0] - dx + 4, 4) * 8 + where_ref[1] * 2 + where_ref[2]
    ones = jnp.ones((TILE, HEAD), jnp.bfloat16)
    row = lax.broadcasted_iota(jnp.int32, (SPAN, TILE), 0)
    lane = lax.broadcasted_iota(jnp.int32, (SPAN, TILE), 1)

    def one_half(half, _):
        rows = pl.ds(pl.multiple_of(half * SPAN, SPAN), SPAN)
        block = jnp.where(half == 0, shard, 63 - shard)
        first = block * SPAN
        low = lax.div(doc_start(first, lens_ref), SPAN) * SPAN
        count = lax.div(first - low, TILE) + 1
        q_tile = jnp.concatenate(
            [q_ref[rows, h * HEAD : (h + 1) * HEAD] for h in range(GROUP)], axis=0
        )
        q_pos = first + row
        q_start = doc_start(q_pos, lens_ref)
        m_scr[...] = jnp.full(m_scr.shape, MASKED, jnp.float32)
        acc_scr[...] = jnp.zeros_like(acc_scr)

        def scores(t, _):
            at = pl.multiple_of(low + t * TILE, SPAN)
            k_pos = at + lane
            bias = jnp.where((k_pos <= q_pos) & (k_pos >= q_start), 0.0, MASKED)
            s = lax.dot_general(
                q_tile,
                kv_ref[pl.ds(at, TILE), :HEAD],
                (((1,), (1,)), ((), ())),
                preferred_element_type=jnp.float32,
            )
            s = (s.reshape(GROUP, SPAN, TILE) + bias[None]).reshape(GROUP * SPAN, TILE)
            s_scr[t] = s
            top = m_scr[...]
            for j in range(TILE // HEAD):
                top = jnp.maximum(top, s[:, j * HEAD : (j + 1) * HEAD])
            m_scr[...] = top
            return 0

        lax.fori_loop(0, count, scores, 0)
        top = jnp.max(m_scr[...], axis=1, keepdims=True)
        m_scr[...] = jnp.broadcast_to(top, m_scr.shape)

        def weigh(t, _):
            at = pl.multiple_of(low + t * TILE, SPAN)
            m = jnp.concatenate([m_scr[...]] * (TILE // HEAD), axis=1)
            w = jnp.exp2(s_scr[t] - m).astype(jnp.bfloat16)
            v_tile = jnp.concatenate([kv_ref[pl.ds(at, TILE), HEAD:], ones], axis=1)
            acc_scr[...] += jnp.dot(w, v_tile, preferred_element_type=jnp.float32)
            return 0

        lax.fori_loop(0, count, weigh, 0)
        out = (acc_scr[:, :HEAD] / acc_scr[:, HEAD:]).astype(jnp.bfloat16)
        for h in range(GROUP):
            o_ref[rows, h * HEAD : (h + 1) * HEAD] = out[h * SPAN : (h + 1) * SPAN]
        return 0

    lax.fori_loop(0, 2, one_half, 0)


def first_kernel(dx, where_ref, lens_ref, q_ref, b0, b1, b2, b3, o_ref, kv_ref, *scratch):
    gather_keys(where_ref, (b0, b1, b2, b3), kv_ref)
    attend_block(where_ref, lens_ref, dx, q_ref, kv_ref, o_ref, *scratch)


def next_kernel(dx, where_ref, lens_ref, q_ref, kv_ref, o_ref, *scratch):
    attend_block(where_ref, lens_ref, dx, q_ref, kv_ref, o_ref, *scratch)


def place_kernel(where_ref, p0, p1, p2, p3, out_ref):
    x = where_ref[0]
    for d, piece in enumerate((p0, p1, p2, p3)):
        start = pl.multiple_of(lax.rem(x + d, 4) * (GROUP * HEAD), GROUP * HEAD)
        out_ref[0, :, pl.ds(start, GROUP * HEAD)] = piece[...]


def layer(queries, keys, values, doc_lengths, interp_num, interp_den):
    bf16 = jnp.bfloat16
    where = jnp.stack([lax.axis_index(a) for a in ("x", "yh", "c")]).astype(jnp.int32)
    smem = pl.BlockSpec(memory_space=pltpu.SMEM)
    vmem = pl.BlockSpec(memory_space=pltpu.VMEM)
    piece = jax.ShapeDtypeStruct((128, GROUP * HEAD), bf16)
    kv, *packed = pl.pallas_call(
        pack_kernel,
        out_shape=(jax.ShapeDtypeStruct((4, 128, 2 * HEAD), bf16),) + (piece,) * 4,
        in_specs=[smem] * 4 + [vmem] * 4,
        out_specs=(vmem,) * 5,
        name="pack",
    )(where, doc_lengths, interp_num, interp_den, frequencies(), queries[0], keys[0], values[0])
    kv = lax.all_to_all(kv, "x", 0, 0, tiled=True)
    near = lax.all_gather(kv, "c", axis=0)
    ring = [(y * 2 + c, (y + 1 - 2 * c) % 4 * 2 + c) for y in range(4) for c in range(2)]
    one_on = lax.ppermute(near, ("yh", "c"), ring)
    core = lax.axis_index("c")
    half = lax.dynamic_index_in_dim(one_on, core, 0, keepdims=False)
    two_on = lax.ppermute(half, ("yh", "c"), ring)
    other = lax.ppermute(one_on, "c", [(0, 1), (1, 0)])
    far = lax.all_gather(two_on, "c", axis=0)
    moved = {0: packed[0]}
    for d in (2, 1, 3):
        moved[d] = lax.ppermute(packed[d], AXES, route(d, 0))
    lengths = jnp.minimum(doc_lengths, TOKENS)
    scratch = [
        pltpu.VMEM((ROUNDS, GROUP * SPAN, TILE), jnp.float32),
        pltpu.VMEM((GROUP * SPAN, HEAD), jnp.float32),
        pltpu.VMEM((GROUP * SPAN, 2 * HEAD), jnp.float32),
    ]
    handed = {}
    ordered = None
    for d in (2, 1, 3, 0):
        if ordered is None:
            result, ordered = pl.pallas_call(
                functools.partial(first_kernel, d),
                out_shape=(piece, jax.ShapeDtypeStruct((TOKENS + TILE, 2 * HEAD), bf16)),
                in_specs=[smem] * 2 + [vmem] * 5,
                out_specs=(vmem, vmem),
                scratch_shapes=scratch,
            )(where, lengths, moved[d], near, one_on, other, far)
        else:
            result = pl.pallas_call(
                functools.partial(next_kernel, d),
                out_shape=piece,
                in_specs=[smem] * 2 + [vmem] * 2,
                out_specs=vmem,
                scratch_shapes=scratch,
            )(where, lengths, moved[d], ordered)
        handed[d] = lax.ppermute(result, AXES, route(-d, 1))
    return pl.pallas_call(
        place_kernel,
        out_shape=jax.ShapeDtypeStruct((1, 128, KV_HEADS * GROUP * HEAD), bf16),
        in_specs=[smem] + [vmem] * 4,
        out_specs=vmem,
        name="place",
    )(where, *(handed[d] for d in range(4)))


def solution(mesh):
    fine = Mesh(mesh.devices.reshape(SIZES), AXES)
    ctx, section = ("x", "yh", "c"), ("yl", "z")
    placed = (
        P(section, ctx, None),
        P(section, ctx, None),
        P(section, ctx, None),
        P(section, None),
        P(),
        P(),
    )
    return jax.shard_map(
        layer, mesh=fine, in_specs=placed, out_specs=P(section, ctx, None), check_vma=False
    )
```

profile of v0, /device:TPU:1, one launch (start us, length us, event | category | flops | bytes accessed | tf_op | source)
XLA Modules:
  0.0 115.8 jit_solution(2070524878542012954)
XLA Ops:
  2.0 3.2 %pack.1 = (bf16[4,128,256]{2,1,0:T(8,128)(2,1)}, bf16[128,1024]{1,0:T(8,128)(2,1)}, bf16[128,1024]{1,0:T(8,128)(2,1)}, bf16[128,1024]{1,0:T(8,128)(2,1)}, bf16[128,1024]{1,0:T(8,128)(2,1)}) custom-call(s32[3]{0:T(128)} %pad_add_fusion.where_ref, s32[1,4]{1,0:T(1,128)} %lens_ref.1, s32[1]{0:T(128)S(6)} %copy.8.num_ref, s32[1]{0:T(128)S(6)} %copy.9.den_ref, ...), custom_call_target="tpu_custom_call" | custom-call | tf_op jit(solution)/shard_map/pack/pallas_call | solution.py:180
  5.2 10.4 %all_to_all.5 = bf16[4,128,256]{2,1,0:T(8,128)(2,1)S(1)} all-to-all(bf16[4,128,256]{2,1,0:T(8,128)(2,1)} %get-tuple-element.14), channel_id=1, replica_groups=mesh['x'=4,'yh'=4,'c'=2,'yl'=2,'z'=12] {'x'}, dimensions={0} | all-to-all | bytes 524288 | tf_op jit(solution)/shard_map/all_to_all | solution.py:187
  15.5 12.0 %all-gather = bf16[8,128,256]{2,1,0:T(8,128)(2,1)S(1)} all-gather(bf16[4,128,256]{2,1,0:T(8,128)(2,1)S(1)} %all_to_all.5), channel_id=2, replica_groups=mesh['x'=4,'yh'=4,'c'=2,'yl'=2,'z'=12] {'c'}, dimensions={0}, use_global_device_ids=true | all-gather | bytes 786432 | tf_op jit(solution)/shard_map/all_gather | solution.py:188
  27.5 1.9 %collective-permute-start.1 = (bf16[2,4,128,256]{3,2,1,0:T(8,128)(2,1)S(1)}, bf16[2,4,128,256]{3,2,1,0:T(8,128)(2,1)S(1)}, u32[]{:S(2)}, u32[]{:S(2)}) collective-permute-start(bf16[2,4,128,256]{3,2,1,0:T(8,128)(2,1)S(1)} %bitcast.10), channel_id=1, source_target_pairs={{0,48},{24,168},{48,96},{72,24},{96,144},{120,72},{144,0},{168,120... | collective-permute-start | bytes 1572872 | tf_op jit(solution)/shard_map/ppermute | solution.py:190
  29.4 9.2 %collective-permute-done.1.b1 = bf16[2,4,128,256]{3,2,1,0:T(8,128)(2,1)S(1)} collective-permute-done((bf16[2,4,128,256]{3,2,1,0:T(8,128)(2,1)S(1)}, bf16[2,4,128,256]{3,2,1,0:T(8,128)(2,1)S(1)}, u32[]{:S(2)}, u32[]{:S(2)}) %collective-permute-start.1) | collective-permute-done | bytes 524320 | tf_op jit(solution)/shard_map/ppermute | solution.py:190
  38.6 5.6 %collective-permute-start.2 = (bf16[2,4,128,256]{3,2,1,0:T(8,128)(2,1)S(1)}, bf16[2,4,128,256]{3,2,1,0:T(8,128)(2,1)S(1)}, u32[]{:S(2)}, u32[]{:S(2)}) collective-permute-start(bf16[2,4,128,256]{3,2,1,0:T(8,128)(2,1)S(1)} %collective-permute-done.1.b1), channel_id=1, source_target_pairs={{0,24},{24,0},{1,25},{25,1},{2,26},{26,2},{3,27},{27,3},{4,28},{28... | collective-permute-start | bytes 1572872 | tf_op jit(solution)/shard_map/ppermute | solution.py:194
  44.3 1.9 %collective-permute-start.3 = (bf16[4,128,256]{2,1,0:T(8,128)(2,1)S(1)}, bf16[4,128,256]{2,1,0:T(8,128)(2,1)S(1)}, u32[]{:S(2)}, u32[]{:S(2)}) collective-permute-start(bf16[4,128,256]{2,1,0:T(8,128)(2,1)S(1)} %dynamic-slice_bitcast_fusion), channel_id=1, source_target_pairs={{0,48},{24,168},{48,96},{72,24},{96,144},{120,72},{144,0},{168,120... | collective-permute-start | bytes 786440 | tf_op jit(solution)/shard_map/ppermute | solution.py:193
  46.2 2.4 %collective-permute-start = (bf16[128,1024]{1,0:T(8,128)(2,1)}, bf16[128,1024]{1,0:T(8,128)(2,1)S(1)}, u32[]{:S(2)}, u32[]{:S(2)}) collective-permute-start(bf16[128,1024]{1,0:T(8,128)(2,1)} %get-tuple-element.13), channel_id=1, source_target_pairs={{0,384},{1,385},{2,386},{3,387},{4,388},{5,389},{6,390},{7,391},{8... | collective-permute-start | bytes 786440 | tf_op jit(solution)/shard_map/ppermute | solution.py:198
  48.7 2.8 %collective-permute-start.5 = (bf16[128,1024]{1,0:T(8,128)(2,1)}, bf16[128,1024]{1,0:T(8,128)(2,1)S(1)}, u32[]{:S(2)}, u32[]{:S(2)}) collective-permute-start(bf16[128,1024]{1,0:T(8,128)(2,1)} %get-tuple-element.16), channel_id=1, source_target_pairs={{0,192},{1,193},{2,194},{3,195},{4,196},{5,197},{6,198},{7,199},{8... | collective-permute-start | bytes 786440 | tf_op jit(solution)/shard_map/ppermute | solution.py:198
  51.5 3.7 %collective-permute-start.8 = (bf16[128,1024]{1,0:T(8,128)(2,1)}, bf16[128,1024]{1,0:T(8,128)(2,1)S(1)}, u32[]{:S(2)}, u32[]{:S(2)}) collective-permute-start(bf16[128,1024]{1,0:T(8,128)(2,1)} %get-tuple-element.18), channel_id=1, source_target_pairs={{0,576},{1,577},{2,578},{3,579},{4,580},{5,581},{6,582},{7,583},{8... | collective-permute-start | bytes 786440 | tf_op jit(solution)/shard_map/ppermute | solution.py:198
  55.7 3.0 %all-gather.1 = bf16[8,128,256]{2,1,0:T(8,128)(2,1)} all-gather(bf16[4,128,256]{2,1,0:T(8,128)(2,1)S(1)} %collective-permute-done.3), channel_id=3, replica_groups=mesh['x'=4,'yh'=4,'c'=2,'yl'=2,'z'=12] {'c'}, dimensions={0}, use_global_device_ids=true | all-gather | bytes 786432 | tf_op jit(solution)/shard_map/all_gather | solution.py:195
  59.6 7.4 %shard_map.73 = (bf16[128,1024]{1,0:T(8,128)(2,1)}, bf16[4608,256]{1,0:T(8,128)(2,1)}) custom-call(s32[3]{0:T(128)} %pad_add_fusion.where_ref, s32[1,4]{1,0:T(1,128)} %broadcast_minimum_fusion.lens_ref, bf16[128,1024]{1,0:T(8,128)(2,1)} %copy-done.5, bf16[2,4,128,256]{3,2,1,0:T(8,128)(2,1)} %bitcast.11, bf16[2,4,128,256]{3,2,1,0:T(8,128)(2,1)} %copy-done.1, ...), custom_call_target="tpu_custom_call" | custom-call | tf_op jit(solution)/shard_map/pallas_call | solution.py:209
  67.0 4.8 %shard_map.74 = bf16[128,1024]{1,0:T(8,128)(2,1)} custom-call(s32[3]{0:T(128)} %pad_add_fusion.where_ref, s32[1,4]{1,0:T(1,128)} %broadcast_minimum_fusion.lens_ref, bf16[128,1024]{1,0:T(8,128)(2,1)} %get-tuple-element.12.q_ref, bf16[4608,256]{1,0:T(8,128)(2,1)} %get-tuple-element.15.kv_ref), custom_call_target="tpu_custom_call" | custom-call | tf_op jit(solution)/shard_map/pallas_call | solution.py:217
  71.9 2.2 %collective-permute-start.4 = (bf16[128,1024]{1,0:T(8,128)(2,1)}, bf16[128,1024]{1,0:T(8,128)(2,1)S(1)}, u32[]{:S(2)}, u32[]{:S(2)}) collective-permute-start(bf16[128,1024]{1,0:T(8,128)(2,1)} %shard_map.74), channel_id=1, source_target_pairs={{0,1},{1,2},{2,3},{3,4},{4,5},{5,6},{6,7},{7,8},{8,9},{9,10},{10,1... | collective-permute-start | bytes 786440 | tf_op jit(solution)/shard_map/ppermute | solution.py:224
  74.1 0.7 copy-done.9
  74.8 6.7 %shard_map.75 = bf16[128,1024]{1,0:T(8,128)(2,1)} custom-call(s32[3]{0:T(128)} %pad_add_fusion.where_ref, s32[1,4]{1,0:T(1,128)} %broadcast_minimum_fusion.lens_ref, bf16[128,1024]{1,0:T(8,128)(2,1)} %copy-done.9, bf16[4608,256]{1,0:T(8,128)(2,1)} %get-tuple-element.15.kv_ref), custom_call_target="tpu_custom_call" | custom-call | tf_op jit(solution)/shard_map/pallas_call | solution.py:217
  81.5 3.4 %collective-permute-start.6 = (bf16[128,1024]{1,0:T(8,128)(2,1)}, bf16[128,1024]{1,0:T(8,128)(2,1)S(1)}, u32[]{:S(2)}, u32[]{:S(2)}) collective-permute-start(bf16[128,1024]{1,0:T(8,128)(2,1)} %shard_map.75), channel_id=1, source_target_pairs={{0,577},{1,578},{2,579},{3,580},{4,581},{5,582},{6,583},{7,584},{8... | collective-permute-start | bytes 786440 | tf_op jit(solution)/shard_map/ppermute | solution.py:224
  84.9 0.7 copy-done.8
  85.6 4.9 %shard_map.76 = bf16[128,1024]{1,0:T(8,128)(2,1)} custom-call(s32[3]{0:T(128)} %pad_add_fusion.where_ref, s32[1,4]{1,0:T(1,128)} %broadcast_minimum_fusion.lens_ref, bf16[128,1024]{1,0:T(8,128)(2,1)} %copy-done.8, bf16[4608,256]{1,0:T(8,128)(2,1)} %get-tuple-element.15.kv_ref), custom_call_target="tpu_custom_call" | custom-call | tf_op jit(solution)/shard_map/pallas_call | solution.py:217
  90.5 4.2 %collective-permute-start.9 = (bf16[128,1024]{1,0:T(8,128)(2,1)}, bf16[128,1024]{1,0:T(8,128)(2,1)S(1)}, u32[]{:S(2)}, u32[]{:S(2)}) collective-permute-start(bf16[128,1024]{1,0:T(8,128)(2,1)} %shard_map.76), channel_id=1, source_target_pairs={{0,193},{1,194},{2,195},{3,196},{4,197},{5,198},{6,199},{7,200},{8... | collective-permute-start | bytes 786440 | tf_op jit(solution)/shard_map/ppermute | solution.py:224
  94.7 7.4 %collective-permute-start.7 = (bf16[128,1024]{1,0:T(8,128)(2,1)S(1)}, bf16[128,1024]{1,0:T(8,128)(2,1)S(1)}, u32[]{:S(2)}, u32[]{:S(2)}) collective-permute-start(bf16[128,1024]{1,0:T(8,128)(2,1)S(1)} %copy-done.11), channel_id=1, source_target_pairs={{0,385},{1,386},{2,387},{3,388},{4,389},{5,390},{6,391},{7,392},{8... | collective-permute-start | bytes 786440 | tf_op jit(solution)/shard_map/ppermute | solution.py:224
  102.2 4.8 %collective-permute-done.9.p3 = bf16[128,1024]{1,0:T(8,128)(2,1)S(1)} collective-permute-done((bf16[128,1024]{1,0:T(8,128)(2,1)}, bf16[128,1024]{1,0:T(8,128)(2,1)S(1)}, u32[]{:S(2)}, u32[]{:S(2)}) %collective-permute-start.9) | collective-permute-done | bytes 262176 | tf_op jit(solution)/shard_map/ppermute | solution.py:224
  107.0 5.9 %collective-permute-done.7.p2 = bf16[128,1024]{1,0:T(8,128)(2,1)S(1)} collective-permute-done((bf16[128,1024]{1,0:T(8,128)(2,1)S(1)}, bf16[128,1024]{1,0:T(8,128)(2,1)S(1)}, u32[]{:S(2)}, u32[]{:S(2)}) %collective-permute-start.7) | collective-permute-done | bytes 262176 | tf_op jit(solution)/shard_map/ppermute | solution.py:224
  113.5 2.2 %place.1 = bf16[1,128,4096]{2,1,0:T(8,128)(2,1)} custom-call(s32[3]{0:T(128)} %pad_add_fusion.where_ref, bf16[128,1024]{1,0:T(8,128)(2,1)} %copy-done.3, bf16[128,1024]{1,0:T(8,128)(2,1)} %copy-done.4, bf16[128,1024]{1,0:T(8,128)(2,1)} %copy-done.7, bf16[128,1024]{1,0:T(8,128)(2,1)} %copy-done.6), custom_call_target="tpu_custom_call" | custom-call | tf_op jit(solution)/shard_map/place/pallas_call | solution.py:225
  (32 shorter events, 2.8 us)
Async XLA Ops:
  0.0 55.2 %copy-start.10 = (s32[1,4]{1,0:T(1,128)S(1)}, s32[1,4]{1,0:T(1,128)}, u32[]{:S(2)}) copy-start(s32[1,4]{1,0:T(1,128)} %lens_ref.1) | copy-start | bytes 52
  27.5 31.2 %copy-start = (bf16[8,128,256]{2,1,0:T(8,128)(2,1)}, bf16[8,128,256]{2,1,0:T(8,128)(2,1)S(1)}, u32[]{:S(2)}) copy-start(bf16[8,128,256]{2,1,0:T(8,128)(2,1)S(1)} %all-gather) | copy-start | bytes 1572868
  27.5 11.1 %collective-permute-start.1 = (bf16[2,4,128,256]{3,2,1,0:T(8,128)(2,1)S(1)}, bf16[2,4,128,256]{3,2,1,0:T(8,128)(2,1)S(1)}, u32[]{:S(2)}, u32[]{:S(2)}) collective-permute-start(bf16[2,4,128,256]{3,2,1,0:T(8,128)(2,1)S(1)} %bitcast.10), channel_id=1, source_target_pairs={{0,48},{24,168},{48,96},{72,24},{96,144},{120,72},{144,0},{168,120... | collective-permute-start | bytes 1572872 | tf_op jit(solution)/shard_map/ppermute | solution.py:190
  38.6 20.1 %copy-start.1 = (bf16[2,4,128,256]{3,2,1,0:T(8,128)(2,1)}, bf16[2,4,128,256]{3,2,1,0:T(8,128)(2,1)S(1)}, u32[]{:S(2)}) copy-start(bf16[2,4,128,256]{3,2,1,0:T(8,128)(2,1)S(1)} %collective-permute-done.1.b1) | copy-start | bytes 1572868
  38.6 20.1 %collective-permute-start.2 = (bf16[2,4,128,256]{3,2,1,0:T(8,128)(2,1)S(1)}, bf16[2,4,128,256]{3,2,1,0:T(8,128)(2,1)S(1)}, u32[]{:S(2)}, u32[]{:S(2)}) collective-permute-start(bf16[2,4,128,256]{3,2,1,0:T(8,128)(2,1)S(1)} %collective-permute-done.1.b1), channel_id=1, source_target_pairs={{0,24},{24,0},{1,25},{25,1},{2,26},{26,2},{3,27},{27,3},{4,28},{28... | collective-permute-start | bytes 1572872 | tf_op jit(solution)/shard_map/ppermute | solution.py:194
  44.3 11.4 %collective-permute-start.3 = (bf16[4,128,256]{2,1,0:T(8,128)(2,1)S(1)}, bf16[4,128,256]{2,1,0:T(8,128)(2,1)S(1)}, u32[]{:S(2)}, u32[]{:S(2)}) collective-permute-start(bf16[4,128,256]{2,1,0:T(8,128)(2,1)S(1)} %dynamic-slice_bitcast_fusion), channel_id=1, source_target_pairs={{0,48},{24,168},{48,96},{72,24},{96,144},{120,72},{144,0},{168,120... | collective-permute-start | bytes 786440 | tf_op jit(solution)/shard_map/ppermute | solution.py:193
  46.2 12.4 %collective-permute-start = (bf16[128,1024]{1,0:T(8,128)(2,1)}, bf16[128,1024]{1,0:T(8,128)(2,1)S(1)}, u32[]{:S(2)}, u32[]{:S(2)}) collective-permute-start(bf16[128,1024]{1,0:T(8,128)(2,1)} %get-tuple-element.13), channel_id=1, source_target_pairs={{0,384},{1,385},{2,386},{3,387},{4,388},{5,389},{6,390},{7,391},{8... | collective-permute-start | bytes 786440 | tf_op jit(solution)/shard_map/ppermute | solution.py:198
  48.7 25.4 %collective-permute-start.5 = (bf16[128,1024]{1,0:T(8,128)(2,1)}, bf16[128,1024]{1,0:T(8,128)(2,1)S(1)}, u32[]{:S(2)}, u32[]{:S(2)}) collective-permute-start(bf16[128,1024]{1,0:T(8,128)(2,1)} %get-tuple-element.16), channel_id=1, source_target_pairs={{0,192},{1,193},{2,194},{3,195},{4,196},{5,197},{6,198},{7,199},{8... | collective-permute-start | bytes 786440 | tf_op jit(solution)/shard_map/ppermute | solution.py:198
  51.5 33.4 %collective-permute-start.8 = (bf16[128,1024]{1,0:T(8,128)(2,1)}, bf16[128,1024]{1,0:T(8,128)(2,1)S(1)}, u32[]{:S(2)}, u32[]{:S(2)}) collective-permute-start(bf16[128,1024]{1,0:T(8,128)(2,1)} %get-tuple-element.18), channel_id=1, source_target_pairs={{0,576},{1,577},{2,578},{3,579},{4,580},{5,581},{6,582},{7,583},{8... | collective-permute-start | bytes 786440 | tf_op jit(solution)/shard_map/ppermute | solution.py:198
  58.7 0.7 copy-start.5
  58.7 0.9 copy-start.2
  71.9 22.8 %copy-start.11 = (bf16[128,1024]{1,0:T(8,128)(2,1)S(1)}, bf16[128,1024]{1,0:T(8,128)(2,1)}, u32[]{:S(2)}) copy-start(bf16[128,1024]{1,0:T(8,128)(2,1)} %get-tuple-element.17) | copy-start | bytes 786436
  71.9 30.2 %collective-permute-start.4 = (bf16[128,1024]{1,0:T(8,128)(2,1)}, bf16[128,1024]{1,0:T(8,128)(2,1)S(1)}, u32[]{:S(2)}, u32[]{:S(2)}) collective-permute-start(bf16[128,1024]{1,0:T(8,128)(2,1)} %shard_map.74), channel_id=1, source_target_pairs={{0,1},{1,2},{2,3},{3,4},{4,5},{5,6},{6,7},{7,8},{8,9},{9,10},{10,1... | collective-permute-start | bytes 786440 | tf_op jit(solution)/shard_map/ppermute | solution.py:224
  74.1 0.7 copy-start.9
  81.5 20.7 %collective-permute-start.6 = (bf16[128,1024]{1,0:T(8,128)(2,1)}, bf16[128,1024]{1,0:T(8,128)(2,1)S(1)}, u32[]{:S(2)}, u32[]{:S(2)}) collective-permute-start(bf16[128,1024]{1,0:T(8,128)(2,1)} %shard_map.75), channel_id=1, source_target_pairs={{0,577},{1,578},{2,579},{3,580},{4,581},{5,582},{6,583},{7,584},{8... | collective-permute-start | bytes 786440 | tf_op jit(solution)/shard_map/ppermute | solution.py:224
  84.9 0.7 copy-start.8
  90.5 16.5 %collective-permute-start.9 = (bf16[128,1024]{1,0:T(8,128)(2,1)}, bf16[128,1024]{1,0:T(8,128)(2,1)S(1)}, u32[]{:S(2)}, u32[]{:S(2)}) collective-permute-start(bf16[128,1024]{1,0:T(8,128)(2,1)} %shard_map.76), channel_id=1, source_target_pairs={{0,193},{1,194},{2,195},{3,196},{4,197},{5,198},{6,199},{7,200},{8... | collective-permute-start | bytes 786440 | tf_op jit(solution)/shard_map/ppermute | solution.py:224
  94.7 18.1 %collective-permute-start.7 = (bf16[128,1024]{1,0:T(8,128)(2,1)S(1)}, bf16[128,1024]{1,0:T(8,128)(2,1)S(1)}, u32[]{:S(2)}, u32[]{:S(2)}) collective-permute-start(bf16[128,1024]{1,0:T(8,128)(2,1)S(1)} %copy-done.11), channel_id=1, source_target_pairs={{0,385},{1,386},{2,387},{3,388},{4,389},{5,390},{6,391},{7,392},{8... | collective-permute-start | bytes 786440 | tf_op jit(solution)/shard_map/ppermute | solution.py:224
  102.1 10.7 %copy-start.3 = (bf16[128,1024]{1,0:T(8,128)(2,1)}, bf16[128,1024]{1,0:T(8,128)(2,1)S(1)}, u32[]{:S(2)}) copy-start(bf16[128,1024]{1,0:T(8,128)(2,1)S(1)} %collective-permute-done.4.p0) | copy-start | bytes 786436
  102.1 10.7 %copy-start.4 = (bf16[128,1024]{1,0:T(8,128)(2,1)}, bf16[128,1024]{1,0:T(8,128)(2,1)S(1)}, u32[]{:S(2)}) copy-start(bf16[128,1024]{1,0:T(8,128)(2,1)S(1)} %collective-permute-done.6.p1) | copy-start | bytes 786436
  107.0 5.9 %copy-start.6 = (bf16[128,1024]{1,0:T(8,128)(2,1)}, bf16[128,1024]{1,0:T(8,128)(2,1)S(1)}, u32[]{:S(2)}) copy-start(bf16[128,1024]{1,0:T(8,128)(2,1)S(1)} %collective-permute-done.9.p3) | copy-start | bytes 786436
  112.9 0.7 copy-start.7
where the time goes:
time: 118 us; the launch traced here: 116 us
  starting transfers between devices  35.6 us (30%)
  Pallas kernels  29.3 us (25%)
  blocking collectives  25.3 us (21%)
  waiting for transfers between devices  19.9 us (17%)
  local copies, waits for them, and re-layouts  3.02 us (3%)
  between operations  1.53 us (1%)
    ppermute x4, starting transfers between devices, layer(): handed[d] = lax.ppermute(result, AXES, route(-d, 1))  17.2 us
    pallas_call x3, Pallas kernels, layer(): pl.pallas_call(functools.partial(next_kernel, d), out_shape=piece, in_spe...  16.4 us
    all_gather x1, blocking collectives, layer(): near = lax.all_gather(kv, 'c', axis=0)  12 us
    ppermute x4, waiting for transfers between devices, layer(): handed[d] = lax.ppermute(result, AXES, route(-d, 1))  10.7 us
    all_to_all x1, blocking collectives, layer(): kv = lax.all_to_all(kv, 'x', 0, 0, tiled=True)  10.4 us
    ppermute x1, waiting for transfers between devices, layer(): one_on = lax.ppermute(near, ('yh', 'c'), ring)  9.19 us
    ppermute x3, starting transfers between devices, layer(): moved[d] = lax.ppermute(packed[d], AXES, route(d, 0))  8.94 us
    pallas_call x1, Pallas kernels, layer(): pl.pallas_call(functools.partial(first_kernel, d), out_shape=(piece, jax....  7.45 us
  transfers between devices with their start and end apart: 10, of which 3 were waited for; matrix products, arithmetic and copies ran while one was open for 0% of the time, Pallas kernels for 21%

commit v1 on v0

v1 whole, which is shorter than its diff:
```python
import functools
import math

import jax
import jax.numpy as jnp
import numpy as np
from jax import lax
from jax.experimental import pallas as pl
from jax.experimental.pallas import tpu as pltpu
from jax.sharding import Mesh, PartitionSpec as P


KV_HEADS = 4
GROUP = 8
HEAD = 128
THETA = 500000.0
MASKED = -1e30
SPAN = 64
TOKENS = 4096
TILE = 512
ROUNDS = 2176 // TILE + 1
SUMS = 16
QUERY_SCALE = math.log2(math.e) / math.sqrt(HEAD)
AXES = ("x", "yh", "c", "yl", "z")
SIZES = (4, 4, 2, 2, 12)


def route(dx, ds):
    pairs = []
    for i in range(math.prod(SIZES)):
        x, yh, c, yl, z = (int(a) for a in np.unravel_index(i, SIZES))
        s = (yl * SIZES[4] + z + ds) % (SIZES[3] * SIZES[4])
        to = ((x + dx) % 4, yh, c, s // SIZES[4], s % SIZES[4])
        pairs.append((i, int(np.ravel_multi_index(to, SIZES))))
    return pairs


def room(mib):
    return pltpu.CompilerParams(vmem_limit_bytes=mib * 2**20)


def held(x):
    return pltpu.with_memory_space_constraint(x, pltpu.VMEM)


def frequencies():
    half = HEAD // 2
    freq = THETA ** (-(2.0 * np.arange(half)) / HEAD)
    return np.concatenate([freq, freq]).astype(np.float32)[None]


def doc_start(position, lens_ref):
    end = 0
    start = jnp.zeros_like(position)
    for d in range(4):
        length = lens_ref[0, d]
        end = end + length
        start = start + jnp.where(position >= end, length, 0)
    return start


def rotation(where_ref, lens_ref, num_ref, den_ref, freq_ref, scale):
    shard = where_ref[0] * 8 + where_ref[1] * 2 + where_ref[2]
    row = lax.broadcasted_iota(jnp.int32, (128, HEAD), 0)
    lane = lax.broadcasted_iota(jnp.int32, (128, HEAD), 1)
    position = jnp.where(row < SPAN, shard * SPAN + row, (63 - shard) * SPAN + row - SPAN)
    offset = (position - doc_start(position, lens_ref)).astype(jnp.float32)
    ratio = jnp.full((128, HEAD), num_ref[0], jnp.int32).astype(jnp.float32) / jnp.full(
        (128, HEAD), den_ref[0], jnp.int32
    ).astype(jnp.float32)
    angle = offset * ratio * freq_ref[...]
    cosine = jnp.cos(angle) * scale
    sine = jnp.sin(angle) * scale
    return cosine, jnp.where(lane < HEAD // 2, -sine, sine)


def turn(part, cosine, sine):
    wide = part.astype(jnp.float32)
    return (wide * cosine + pltpu.roll(wide, HEAD // 2, 1) * sine).astype(jnp.bfloat16)


def pack_keys_kernel(where_ref, lens_ref, num_ref, den_ref, freq_ref, k_ref, v_ref, kv_ref):
    cosine, sine = rotation(where_ref, lens_ref, num_ref, den_ref, freq_ref, 1.0)
    for h in range(KV_HEADS):
        cols = slice(h * HEAD, (h + 1) * HEAD)
        kv_ref[h, :, :HEAD] = turn(k_ref[:, cols], cosine, sine)
        kv_ref[h, :, HEAD:] = v_ref[:, cols].T


def pack_queries_kernel(where_ref, lens_ref, num_ref, den_ref, freq_ref, q_ref, *q_out):
    cosine, sine = rotation(where_ref, lens_ref, num_ref, den_ref, freq_ref, QUERY_SCALE)
    for d in range(4):
        group = lax.rem(where_ref[0] + d, 4)
        for h in range(GROUP):
            start = pl.multiple_of(group * (GROUP * HEAD) + h * HEAD, HEAD)
            q_out[d][:, h * HEAD : (h + 1) * HEAD] = turn(q_ref[:, pl.ds(start, HEAD)], cosine, sine)


def gather_keys(where_ref, blocks, k_ref, vt_ref):
    yh, core = where_ref[1], where_ref[2]
    sides = (0, 2 * core - 1, 1 - 2 * core, 2)
    for block, side in zip(blocks, sides):
        y = lax.rem(yh + side + 4, 4)
        for x in range(4):
            early = pl.multiple_of((x * 8 + y * 2) * SPAN, 2 * SPAN)
            late = pl.multiple_of((62 - x * 8 - y * 2) * SPAN, 2 * SPAN)
            k_ref[pl.ds(early, 2 * SPAN), :] = jnp.concatenate(
                [block[0, x, :SPAN, :HEAD], block[1, x, :SPAN, :HEAD]], axis=0
            )
            k_ref[pl.ds(late, 2 * SPAN), :] = jnp.concatenate(
                [block[1, x, SPAN:, :HEAD], block[0, x, SPAN:, :HEAD]], axis=0
            )
            a, b = block[0, x, :, HEAD:], block[1, x, :, HEAD:]
            vt_ref[:HEAD, pl.ds(early, 2 * SPAN)] = jnp.concatenate([a[:, :SPAN], b[:, :SPAN]], axis=1)
            vt_ref[:HEAD, pl.ds(late, 2 * SPAN)] = jnp.concatenate([b[:, SPAN:], a[:, SPAN:]], axis=1)
    k_ref[TOKENS:, :] = jnp.zeros((TILE, HEAD), jnp.bfloat16)
    vt_ref[:HEAD, TOKENS:] = jnp.zeros((HEAD, TILE), jnp.bfloat16)
    vt_ref[HEAD:, :] = jnp.ones((SUMS, TOKENS + TILE), jnp.bfloat16)


def attend_block(where_ref, lens_ref, dx, q_ref, k_ref, vt_ref, o_ref, s_scr, m_scr, acc_scr):
    shard = lax.rem(where_ref[0] - dx + 4, 4) * 8 + where_ref[1] * 2 + where_ref[2]
    width = GROUP * SPAN
    key = lax.broadcasted_iota(jnp.int32, (TILE, HEAD), 0)
    token = lax.rem(lax.broadcasted_iota(jnp.int32, (8, HEAD), 1), SPAN)

    def one_half(half, _):
        rows = pl.ds(pl.multiple_of(half * SPAN, SPAN), SPAN)
        block = jnp.where(half == 0, shard, 63 - shard)
        first = block * SPAN
        low = lax.div(doc_start(first, lens_ref), HEAD) * HEAD
        count = lax.div(first - low, TILE) + 1
        q_tile = jnp.concatenate(
            [q_ref[rows, h * HEAD : (h + 1) * HEAD] for h in range(GROUP)], axis=0
        )
        q_pos = first + token
        q_start = doc_start(q_pos, lens_ref)
        m_scr[...] = jnp.full(m_scr.shape, MASKED, jnp.float32)
        acc_scr[...] = jnp.zeros_like(acc_scr)

        def scores(t, _):
            at = pl.multiple_of(low + t * TILE, HEAD)
            bias = jnp.where(
                (key <= (q_pos - at)[:1]) & (key >= (q_start - at)[:1]), 0.0, MASKED
            )
            s = lax.dot_general(
                k_ref[pl.ds(at, TILE), :],
                q_tile,
                (((1,), (1,)), ((), ())),
                preferred_element_type=jnp.float32,
            )
            s = s + jnp.concatenate([bias] * (width // HEAD), axis=1)
            s_scr[t] = s
            m_scr[...] = jnp.maximum(m_scr[...], jnp.max(s.reshape(TILE // 8, 8, width), axis=0))
            return 0

        lax.fori_loop(0, count, scores, 0)
        m_scr[...] = jnp.broadcast_to(jnp.max(m_scr[...], axis=0, keepdims=True), m_scr.shape)

        def weigh(t, _):
            at = pl.multiple_of(low + t * TILE, HEAD)
            s = s_scr[t].reshape(TILE // 8, 8, width) - m_scr[...][None]
            w = jnp.exp2(s).reshape(TILE, width).astype(jnp.bfloat16)
            acc_scr[...] += jnp.dot(
                vt_ref[:, pl.ds(at, TILE)], w, preferred_element_type=jnp.float32
            )
            return 0

        lax.fori_loop(0, count, weigh, 0)
        out = (acc_scr[:HEAD, :] * (1.0 / acc_scr[HEAD : HEAD + 1, :])).T.astype(jnp.bfloat16)
        for h in range(GROUP):
            o_ref[rows, h * HEAD : (h + 1) * HEAD] = out[h * SPAN : (h + 1) * SPAN]
        return 0

    lax.fori_loop(0, 2, one_half, 0)


def first_kernel(dx, where_ref, lens_ref, q_ref, b0, b1, b2, b3, o_ref, k_ref, vt_ref, *scratch):
    gather_keys(where_ref, (b0, b1, b2, b3), k_ref, vt_ref)
    attend_block(where_ref, lens_ref, dx, q_ref, k_ref, vt_ref, o_ref, *scratch)


def next_kernel(dx, where_ref, lens_ref, q_ref, k_ref, vt_ref, o_ref, *scratch):
    attend_block(where_ref, lens_ref, dx, q_ref, k_ref, vt_ref, o_ref, *scratch)


def first_place_kernel(col_ref, piece_ref, out_ref):
    out_ref[0] = piece_ref[...]


def next_place_kernel(col_ref, piece_ref, old_ref, out_ref):
    out_ref[0] = piece_ref[...]


def place(piece, out, column):
    width = GROUP * HEAD
    first = out is None
    return pl.pallas_call(
        first_place_kernel if first else next_place_kernel,
        out_shape=jax.ShapeDtypeStruct((1, 128, KV_HEADS * width), jnp.bfloat16),
        grid_spec=pltpu.PrefetchScalarGridSpec(
            num_scalar_prefetch=1,
            grid=(1,),
            in_specs=[pl.BlockSpec((128, width), lambda i, col: (0, 0))]
            + ([] if first else [pl.BlockSpec(memory_space=pl.ANY)]),
            out_specs=pl.BlockSpec((1, 128, width), lambda i, col: (0, 0, col[0])),
        ),
        input_output_aliases={} if first else {2: 0},
        compiler_params=room(4),
    )(*((column, held(piece)) if first else (column, held(piece), out)))


def layer(queries, keys, values, doc_lengths, interp_num, interp_den):
    bf16 = jnp.bfloat16
    where = jnp.stack([lax.axis_index(a) for a in ("x", "yh", "c")]).astype(jnp.int32)
    smem = pl.BlockSpec(memory_space=pltpu.SMEM)
    vmem = pl.BlockSpec(memory_space=pltpu.VMEM)
    piece = pltpu.VMEM((128, GROUP * HEAD), bf16)
    turning = (where, doc_lengths, interp_num, interp_den, frequencies())
    kv = pl.pallas_call(
        pack_keys_kernel,
        out_shape=pltpu.VMEM((4, 128, 2 * HEAD), bf16),
        in_specs=[smem] * 4 + [vmem] * 3,
        out_specs=vmem,
        name="pack_keys",
        compiler_params=room(12),
    )(*turning, keys[0], values[0])
    packed = pl.pallas_call(
        pack_queries_kernel,
        out_shape=(piece,) * 4,
        in_specs=[smem] * 4 + [vmem] * 2,
        out_specs=(vmem,) * 4,
        name="pack_queries",
        compiler_params=room(12),
    )(*turning, queries[0])
    kv = lax.all_to_all(kv, "x", 0, 0, tiled=True)
    near = lax.all_gather(kv, "c", axis=0)
    ring = [(y * 2 + c, (y + 1 - 2 * c) % 4 * 2 + c) for y in range(4) for c in range(2)]
    one_on = lax.ppermute(near, ("yh", "c"), ring)
    core = lax.axis_index("c")
    half = lax.dynamic_index_in_dim(one_on, core, 0, keepdims=False)
    two_on = lax.ppermute(half, ("yh", "c"), ring)
    other = lax.ppermute(one_on, "c", [(0, 1), (1, 0)])
    far = lax.all_gather(two_on, "c", axis=0)
    moved = {0: packed[0]}
    for d in (2, 1, 3):
        moved[d] = lax.ppermute(packed[d], AXES, route(d, 0))
    lengths = jnp.minimum(doc_lengths, TOKENS)
    scratch = [
        pltpu.VMEM((ROUNDS, TILE, GROUP * SPAN), jnp.float32),
        pltpu.VMEM((8, GROUP * SPAN), jnp.float32),
        pltpu.VMEM((HEAD + SUMS, GROUP * SPAN), jnp.float32),
    ]
    laid_out = (
        pltpu.VMEM((TOKENS + TILE, HEAD), bf16),
        pltpu.VMEM((HEAD + SUMS, TOKENS + TILE), bf16),
    )
    handed = {}
    ordered = None
    for d in (2, 1, 3, 0):
        if ordered is None:
            result, *ordered = pl.pallas_call(
                functools.partial(first_kernel, d),
                out_shape=(piece,) + laid_out,
                in_specs=[smem] * 2 + [vmem] * 5,
                out_specs=(vmem,) * 3,
                scratch_shapes=scratch,
                compiler_params=room(24),
            )(where, lengths, *map(held, (moved[d], near, one_on, other, far)))
        else:
            result = pl.pallas_call(
                functools.partial(next_kernel, d),
                out_shape=piece,
                in_specs=[smem] * 2 + [vmem] * 3,
                out_specs=vmem,
                scratch_shapes=scratch,
                compiler_params=room(24),
            )(where, lengths, *map(held, (moved[d], *ordered)))
        handed[d] = lax.ppermute(result, AXES, route(-d, 1))
    out = None
    for d in (2, 1, 3, 0):
        out = place(handed[d], out, (where[:1] + d) % 4)
    return out


def solution(mesh):
    fine = Mesh(mesh.devices.reshape(SIZES), AXES)
    ctx, section = ("x", "yh", "c"), ("yl", "z")
    placed = (
        P(section, ctx, None),
        P(section, ctx, None),
        P(section, ctx, None),
        P(section, None),
        P(),
        P(),
    )
    return jax.shard_map(
        layer, mesh=fine, in_specs=placed, out_specs=P(section, ctx, None), check_vma=False
    )
```

time: 118 us -> 110 us (0.932); the launches traced: 116 us -> 109 us
  Pallas kernels: 29.3 us -> 20.5 us
  waiting for transfers between devices: 19.9 us -> 26.4 us
  starting transfers between devices: 35.6 us -> 33.5 us
  blocking collectives: 25.3 us -> 24 us
    pallas_call x3, Pallas kernels: 16.4 us -> 10.2 us  [layer(): pl.pallas_call(functools.partial(next_kernel, d), out_shape=piece, in_spe...]
    ppermute x4, waiting for transfers between devices: 10.7 us -> 16.1 us  [layer(): handed[d] = lax.ppermute(result, AXES, route(-d, 1))]
    pallas_call x3 -> x7, Pallas kernels: 12.9 us -> 10.3 us  [the longest x1 5.1 us: layer(): pl.pallas_call(functools.partial(first_kernel, d), out_shape=(piece,) + l...]
    ppermute x4, starting transfers between devices: 17.2 us -> 15 us  [layer(): handed[d] = lax.ppermute(result, AXES, route(-d, 1))]
    unnamed x24 -> x14, local copies, waits for them, and re-layouts: 2.99 us -> 3.13 us
  transfers between devices with their start and end apart: 10 -> 10, of which waited for: 3 -> 5; matrix products, arithmetic and copies ran while one was open for 0% -> 0% of each run, Pallas kernels for 21% -> 17%
where the time goes in v1:
time: 110 us; the launch traced here: 109 us
  starting transfers between devices  33.5 us (30%)
  waiting for transfers between devices  26.4 us (24%)
  blocking collectives  24 us (22%)
  Pallas kernels  20.5 us (19%)
  local copies, waits for them, and re-layouts  3.16 us (3%)
  between operations  1.62 us (1%)
    ppermute x4, waiting for transfers between devices, layer(): handed[d] = lax.ppermute(result, AXES, route(-d, 1))  16.1 us
    ppermute x4, starting transfers between devices, layer(): handed[d] = lax.ppermute(result, AXES, route(-d, 1))  15 us
    all_gather x1, blocking collectives, layer(): near = lax.all_gather(kv, 'c', axis=0)  11.2 us
    pallas_call x3, Pallas kernels, layer(): pl.pallas_call(functools.partial(next_kernel, d), out_shape=piece, in_spe...  10.2 us
    all_to_all x1, blocking collectives, layer(): kv = lax.all_to_all(kv, 'x', 0, 0, tiled=True)  10.2 us
    ppermute x1, waiting for transfers between devices, layer(): one_on = lax.ppermute(near, ('yh', 'c'), ring)  9.82 us
    ppermute x3, starting transfers between devices, layer(): moved[d] = lax.ppermute(packed[d], AXES, route(d, 0))  8.94 us
    ppermute x1, starting transfers between devices, layer(): other = lax.ppermute(one_on, 'c', [(0, 1), (1, 0)])  5.8 us
  transfers between devices with their start and end apart: 10, of which 5 were waited for; matrix products, arithmetic and copies ran while one was open for 0% of the time, Pallas kernels for 17%

profile of v1, /device:TPU:1, one launch (start us, length us, event | category | flops | bytes accessed | tf_op | source)
XLA Modules:
  0.0 109.4 jit_solution(18436898364681508998)
XLA Ops:
  1.5 0.9 copy-done.1
  2.4 0.9 copy-done.2
  5.5 10.2 %all_to_all.5 = bf16[4,128,256]{2,1,0:T(8,128)(2,1)S(1)} all-to-all(bf16[4,128,256]{2,1,0:T(8,128)(2,1)S(1)} %pack_keys.1), channel_id=1, replica_groups=mesh['x'=4,'yh'=4,'c'=2,'yl'=2,'z'=12] {'x'}, dimensions={0} | all-to-all | bytes 524288 | tf_op jit(solution)/shard_map/all_to_all | solution.py:236
  15.7 11.2 %all-gather = bf16[8,128,256]{2,1,0:T(8,128)(2,1)S(1)} all-gather(bf16[4,128,256]{2,1,0:T(8,128)(2,1)S(1)} %all_to_all.5), channel_id=2, replica_groups=mesh['x'=4,'yh'=4,'c'=2,'yl'=2,'z'=12] {'c'}, dimensions={0}, use_global_device_ids=true | all-gather | bytes 786432 | tf_op jit(solution)/shard_map/all_gather | solution.py:237
  26.8 1.9 %collective-permute-start.1 = (bf16[2,4,128,256]{3,2,1,0:T(8,128)(2,1)S(1)}, bf16[2,4,128,256]{3,2,1,0:T(8,128)(2,1)S(1)}, u32[]{:S(2)}, u32[]{:S(2)}) collective-permute-start(bf16[2,4,128,256]{3,2,1,0:T(8,128)(2,1)S(1)} %bitcast.10), channel_id=1, source_target_pairs={{0,48},{24,168},{48,96},{72,24},{96,144},{120,72},{144,0},{168,120... | collective-permute-start | bytes 1572872 | tf_op jit(solution)/shard_map/ppermute | solution.py:239
  28.8 9.8 %collective-permute-done.1.b1 = bf16[2,4,128,256]{3,2,1,0:T(8,128)(2,1)S(1)} collective-permute-done((bf16[2,4,128,256]{3,2,1,0:T(8,128)(2,1)S(1)}, bf16[2,4,128,256]{3,2,1,0:T(8,128)(2,1)S(1)}, u32[]{:S(2)}, u32[]{:S(2)}) %collective-permute-start.1) | collective-permute-done | bytes 524320 | tf_op jit(solution)/shard_map/ppermute | solution.py:239
  38.6 5.8 %collective-permute-start.2 = (bf16[2,4,128,256]{3,2,1,0:T(8,128)(2,1)S(1)}, bf16[2,4,128,256]{3,2,1,0:T(8,128)(2,1)S(1)}, u32[]{:S(2)}, u32[]{:S(2)}) collective-permute-start(bf16[2,4,128,256]{3,2,1,0:T(8,128)(2,1)S(1)} %collective-permute-done.1.b1), channel_id=1, source_target_pairs={{0,24},{24,0},{1,25},{25,1},{2,26},{26,2},{3,27},{27,3},{4,28},{28... | collective-permute-start | bytes 1572872 | tf_op jit(solution)/shard_map/ppermute | solution.py:243
  44.4 1.9 %collective-permute-start.3 = (bf16[4,128,256]{2,1,0:T(8,128)(2,1)S(1)}, bf16[4,128,256]{2,1,0:T(8,128)(2,1)S(1)}, u32[]{:S(2)}, u32[]{:S(2)}) collective-permute-start(bf16[4,128,256]{2,1,0:T(8,128)(2,1)S(1)} %dynamic-slice_bitcast_fusion), channel_id=1, source_target_pairs={{0,48},{24,168},{48,96},{72,24},{96,144},{120,72},{144,0},{168,120... | collective-permute-start | bytes 786440 | tf_op jit(solution)/shard_map/ppermute | solution.py:242
  46.4 1.4 %pack_queries.1 = (bf16[128,1024]{1,0:T(8,128)(2,1)S(1)}, bf16[128,1024]{1,0:T(8,128)(2,1)S(1)}, bf16[128,1024]{1,0:T(8,128)(2,1)S(1)}, bf16[128,1024]{1,0:T(8,128)(2,1)S(1)}) custom-call(s32[3]{0:T(128)S(1)} %pad_add_fusion.where_ref, s32[1,4]{1,0:T(1,128)S(1)} %copy-done.4, s32[1]{0:T(128)S(6)} %copy.14.num_ref, s32[1]{0:T(128)S(6)} %copy.15.den_ref, ...), custom_call_target="tpu_custom_call" | custom-call | tf_op jit(solution)/shard_map/pack_queries/pallas_call | solution.py:228
  47.8 2.4 %collective-permute-start = (bf16[128,1024]{1,0:T(8,128)(2,1)S(1)}, bf16[128,1024]{1,0:T(8,128)(2,1)S(1)}, u32[]{:S(2)}, u32[]{:S(2)}) collective-permute-start(bf16[128,1024]{1,0:T(8,128)(2,1)S(1)} %get-tuple-element.13), channel_id=1, source_target_pairs={{0,384},{1,385},{2,386},{3,387},{4,388},{5,389},{6,390},{7,391},{8... | collective-permute-start | bytes 786440 | tf_op jit(solution)/shard_map/ppermute | solution.py:247
  50.3 2.8 %collective-permute-start.7 = (bf16[128,1024]{1,0:T(8,128)(2,1)S(1)}, bf16[128,1024]{1,0:T(8,128)(2,1)S(1)}, u32[]{:S(2)}, u32[]{:S(2)}) collective-permute-start(bf16[128,1024]{1,0:T(8,128)(2,1)S(1)} %get-tuple-element.17), channel_id=1, source_target_pairs={{0,192},{1,193},{2,194},{3,195},{4,196},{5,197},{6,198},{7,199},{8... | collective-permute-start | bytes 786440 | tf_op jit(solution)/shard_map/ppermute | solution.py:247
  53.1 3.7 %collective-permute-start.5 = (bf16[128,1024]{1,0:T(8,128)(2,1)S(1)}, bf16[128,1024]{1,0:T(8,128)(2,1)S(1)}, u32[]{:S(2)}, u32[]{:S(2)}) collective-permute-start(bf16[128,1024]{1,0:T(8,128)(2,1)S(1)} %get-tuple-element.16), channel_id=1, source_target_pairs={{0,576},{1,577},{2,578},{3,579},{4,580},{5,581},{6,582},{7,583},{8... | collective-permute-start | bytes 786440 | tf_op jit(solution)/shard_map/ppermute | solution.py:247
  56.8 2.7 %all-gather.1 = bf16[8,128,256]{2,1,0:T(8,128)(2,1)S(1)} all-gather(bf16[4,128,256]{2,1,0:T(8,128)(2,1)S(1)} %collective-permute-done.3), channel_id=3, replica_groups=mesh['x'=4,'yh'=4,'c'=2,'yl'=2,'z'=12] {'c'}, dimensions={0}, use_global_device_ids=true | all-gather | bytes 786432 | tf_op jit(solution)/shard_map/all_gather | solution.py:244
  59.4 5.1 %shard_map.73 = (bf16[128,1024]{1,0:T(8,128)(2,1)S(1)}, bf16[4608,128]{1,0:T(8,128)(2,1)S(1)}, bf16[144,4608]{1,0:T(8,128)(2,1)S(1)}) custom-call(s32[3]{0:T(128)S(1)} %pad_add_fusion.where_ref, s32[1,4]{1,0:T(1,128)S(1)} %broadcast_minimum_fusion.lens_ref, bf16[128,1024]{1,0:T(8,128)(2,1)S(1)} %collective-permute-done.q_ref, ...), custom_call_target="tpu_custom_call" | custom-call | tf_op jit(solution)/shard_map/pallas_call | solution.py:262
  65.1 4.7 %shard_map.76 = bf16[128,1024]{1,0:T(8,128)(2,1)S(1)} custom-call(s32[3]{0:T(128)S(1)} %pad_add_fusion.where_ref, s32[1,4]{1,0:T(1,128)S(1)} %broadcast_minimum_fusion.lens_ref, bf16[128,1024]{1,0:T(8,128)(2,1)S(1)} %collective-permute-done.7.q_ref, bf16[4608,128]{1,0:T(8,128)(2,1)S(1)} %get-tuple-element.14.k_ref, ...), custom_call_target="tpu_custom_call" | custom-call | tf_op jit(solution)/shard_map/pallas_call | solution.py:271
  69.8 2.6 %collective-permute-start.8 = (bf16[128,1024]{1,0:T(8,128)(2,1)S(1)}, bf16[128,1024]{1,0:T(8,128)(2,1)S(1)}, u32[]{:S(2)}, u32[]{:S(2)}) collective-permute-start(bf16[128,1024]{1,0:T(8,128)(2,1)S(1)} %shard_map.76), channel_id=1, source_target_pairs={{0,577},{1,578},{2,579},{3,580},{4,581},{5,582},{6,583},{7,584},{8... | collective-permute-start | bytes 786440 | tf_op jit(solution)/shard_map/ppermute | solution.py:279
  72.3 3.6 %collective-permute-start.9 = (bf16[128,1024]{1,0:T(8,128)(2,1)S(1)}, bf16[128,1024]{1,0:T(8,128)(2,1)S(1)}, u32[]{:S(2)}, u32[]{:S(2)}) collective-permute-start(bf16[128,1024]{1,0:T(8,128)(2,1)S(1)} %get-tuple-element.18), channel_id=1, source_target_pairs={{0,385},{1,386},{2,387},{3,388},{4,389},{5,390},{6,391},{7,392},{8... | collective-permute-start | bytes 786440 | tf_op jit(solution)/shard_map/ppermute | solution.py:279
  75.9 2.8 %shard_map.75 = bf16[128,1024]{1,0:T(8,128)(2,1)S(1)} custom-call(s32[3]{0:T(128)S(1)} %pad_add_fusion.where_ref, s32[1,4]{1,0:T(1,128)S(1)} %broadcast_minimum_fusion.lens_ref, bf16[128,1024]{1,0:T(8,128)(2,1)S(1)} %collective-permute-done.5.q_ref, bf16[4608,128]{1,0:T(8,128)(2,1)S(1)} %get-tuple-element.14.k_ref, ...), custom_call_target="tpu_custom_call" | custom-call | tf_op jit(solution)/shard_map/pallas_call | solution.py:271
  78.7 5.6 %collective-permute-start.6 = (bf16[128,1024]{1,0:T(8,128)(2,1)S(1)}, bf16[128,1024]{1,0:T(8,128)(2,1)S(1)}, u32[]{:S(2)}, u32[]{:S(2)}) collective-permute-start(bf16[128,1024]{1,0:T(8,128)(2,1)S(1)} %shard_map.75), channel_id=1, source_target_pairs={{0,193},{1,194},{2,195},{3,196},{4,197},{5,198},{6,199},{7,200},{8... | collective-permute-start | bytes 786440 | tf_op jit(solution)/shard_map/ppermute | solution.py:279
  84.3 2.8 %shard_map.74 = bf16[128,1024]{1,0:T(8,128)(2,1)S(1)} custom-call(s32[3]{0:T(128)S(1)} %pad_add_fusion.where_ref, s32[1,4]{1,0:T(1,128)S(1)} %broadcast_minimum_fusion.lens_ref, bf16[128,1024]{1,0:T(8,128)(2,1)S(1)} %get-tuple-element.12.q_ref, bf16[4608,128]{1,0:T(8,128)(2,1)S(1)} %get-tuple-element.14.k_ref, bf16[144,4608]{1,0:T(8,128)(2,1)S(1)} %get-tuple-element.15.vt_ref), custom_call_target="tpu_custom_call" | custom-call | tf_op jit(solution)/shard_map/pallas_call | solution.py:271
  87.1 3.3 %collective-permute-start.4 = (bf16[128,1024]{1,0:T(8,128)(2,1)S(1)}, bf16[128,1024]{1,0:T(8,128)(2,1)S(1)}, u32[]{:S(2)}, u32[]{:S(2)}) collective-permute-start(bf16[128,1024]{1,0:T(8,128)(2,1)S(1)} %shard_map.74), channel_id=1, source_target_pairs={{0,1},{1,2},{2,3},{3,4},{4,5},{5,6},{6,7},{7,8},{8,9},{9,10},{10,1... | collective-permute-start | bytes 786440 | tf_op jit(solution)/shard_map/ppermute | solution.py:279
  90.4 3.1 %collective-permute-done.9.piece_ref = bf16[128,1024]{1,0:T(8,128)(2,1)S(1)} collective-permute-done((bf16[128,1024]{1,0:T(8,128)(2,1)S(1)}, bf16[128,1024]{1,0:T(8,128)(2,1)S(1)}, u32[]{:S(2)}, u32[]{:S(2)}) %collective-permute-start.9) | collective-permute-done | bytes 262176 | tf_op jit(solution)/shard_map/ppermute | solution.py:279
  94.9 5.3 %collective-permute-done.6.piece_ref = bf16[128,1024]{1,0:T(8,128)(2,1)S(1)} collective-permute-done((bf16[128,1024]{1,0:T(8,128)(2,1)S(1)}, bf16[128,1024]{1,0:T(8,128)(2,1)S(1)}, u32[]{:S(2)}, u32[]{:S(2)}) %collective-permute-start.6) | collective-permute-done | bytes 262176 | tf_op jit(solution)/shard_map/ppermute | solution.py:279
  100.9 7.8 %collective-permute-done.4.piece_ref = bf16[128,1024]{1,0:T(8,128)(2,1)S(1)} collective-permute-done((bf16[128,1024]{1,0:T(8,128)(2,1)S(1)}, bf16[128,1024]{1,0:T(8,128)(2,1)S(1)}, u32[]{:S(2)}, u32[]{:S(2)}) %collective-permute-start.4) | collective-permute-done | bytes 262176 | tf_op jit(solution)/shard_map/ppermute | solution.py:279
  (26 shorter events, 5.7 us)
Async XLA Ops:
  0.0 46.3 %copy-start.6 = (f32[1,128]{1,0:T(1,128)S(1)}, f32[1,128]{1,0:T(1,128)}, u32[]{:S(2)}) copy-start(f32[1,128]{1,0:T(1,128)} %constant.68.clone.freq_ref) | copy-start | bytes 1540
  0.0 46.4 %copy-start = (bf16[1,128,4096]{2,1,0:T(8,128)(2,1)S(1)}, bf16[1,128,4096]{2,1,0:T(8,128)(2,1)}, u32[]{:S(2)}) copy-start(bf16[1,128,4096]{2,1,0:T(8,128)(2,1)} %param.7) | copy-start | bytes 3145732
  1.5 0.9 copy-start.1
  2.4 0.9 copy-start.2
  3.3 0.7 copy-start.3
  3.9 0.7 copy-start.5
  4.6 41.8 %copy-start.4 = (s32[1,4]{1,0:T(1,128)S(1)}, s32[1,4]{1,0:T(1,128)}, u32[]{:S(2)}) copy-start(s32[1,4]{1,0:T(1,128)} %lens_ref.3) | copy-start | bytes 52
  26.8 11.7 %collective-permute-start.1 = (bf16[2,4,128,256]{3,2,1,0:T(8,128)(2,1)S(1)}, bf16[2,4,128,256]{3,2,1,0:T(8,128)(2,1)S(1)}, u32[]{:S(2)}, u32[]{:S(2)}) collective-permute-start(bf16[2,4,128,256]{3,2,1,0:T(8,128)(2,1)S(1)} %bitcast.10), channel_id=1, source_target_pairs={{0,48},{24,168},{48,96},{72,24},{96,144},{120,72},{144,0},{168,120... | collective-permute-start | bytes 1572872 | tf_op jit(solution)/shard_map/ppermute | solution.py:239
  38.6 20.9 %collective-permute-start.2 = (bf16[2,4,128,256]{3,2,1,0:T(8,128)(2,1)S(1)}, bf16[2,4,128,256]{3,2,1,0:T(8,128)(2,1)S(1)}, u32[]{:S(2)}, u32[]{:S(2)}) collective-permute-start(bf16[2,4,128,256]{3,2,1,0:T(8,128)(2,1)S(1)} %collective-permute-done.1.b1), channel_id=1, source_target_pairs={{0,24},{24,0},{1,25},{25,1},{2,26},{26,2},{3,27},{27,3},{4,28},{28... | collective-permute-start | bytes 1572872 | tf_op jit(solution)/shard_map/ppermute | solution.py:243
  44.4 12.4 %collective-permute-start.3 = (bf16[4,128,256]{2,1,0:T(8,128)(2,1)S(1)}, bf16[4,128,256]{2,1,0:T(8,128)(2,1)S(1)}, u32[]{:S(2)}, u32[]{:S(2)}) collective-permute-start(bf16[4,128,256]{2,1,0:T(8,128)(2,1)S(1)} %dynamic-slice_bitcast_fusion), channel_id=1, source_target_pairs={{0,48},{24,168},{48,96},{72,24},{96,144},{120,72},{144,0},{168,120... | collective-permute-start | bytes 786440 | tf_op jit(solution)/shard_map/ppermute | solution.py:242
  47.8 11.7 %collective-permute-start = (bf16[128,1024]{1,0:T(8,128)(2,1)S(1)}, bf16[128,1024]{1,0:T(8,128)(2,1)S(1)}, u32[]{:S(2)}, u32[]{:S(2)}) collective-permute-start(bf16[128,1024]{1,0:T(8,128)(2,1)S(1)} %get-tuple-element.13), channel_id=1, source_target_pairs={{0,384},{1,385},{2,386},{3,387},{4,388},{5,389},{6,390},{7,391},{8... | collective-permute-start | bytes 786440 | tf_op jit(solution)/shard_map/ppermute | solution.py:247
  50.3 14.8 %collective-permute-start.7 = (bf16[128,1024]{1,0:T(8,128)(2,1)S(1)}, bf16[128,1024]{1,0:T(8,128)(2,1)S(1)}, u32[]{:S(2)}, u32[]{:S(2)}) collective-permute-start(bf16[128,1024]{1,0:T(8,128)(2,1)S(1)} %get-tuple-element.17), channel_id=1, source_target_pairs={{0,192},{1,193},{2,194},{3,195},{4,196},{5,197},{6,198},{7,199},{8... | collective-permute-start | bytes 786440 | tf_op jit(solution)/shard_map/ppermute | solution.py:247
  53.1 22.8 %collective-permute-start.5 = (bf16[128,1024]{1,0:T(8,128)(2,1)S(1)}, bf16[128,1024]{1,0:T(8,128)(2,1)S(1)}, u32[]{:S(2)}, u32[]{:S(2)}) collective-permute-start(bf16[128,1024]{1,0:T(8,128)(2,1)S(1)} %get-tuple-element.16), channel_id=1, source_target_pairs={{0,576},{1,577},{2,578},{3,579},{4,580},{5,581},{6,582},{7,583},{8... | collective-permute-start | bytes 786440 | tf_op jit(solution)/shard_map/ppermute | solution.py:247
  69.8 24.4 %collective-permute-start.8 = (bf16[128,1024]{1,0:T(8,128)(2,1)S(1)}, bf16[128,1024]{1,0:T(8,128)(2,1)S(1)}, u32[]{:S(2)}, u32[]{:S(2)}) collective-permute-start(bf16[128,1024]{1,0:T(8,128)(2,1)S(1)} %shard_map.76), channel_id=1, source_target_pairs={{0,577},{1,578},{2,579},{3,580},{4,581},{5,582},{6,583},{7,584},{8... | collective-permute-start | bytes 786440 | tf_op jit(solution)/shard_map/ppermute | solution.py:279
  72.3 21.1 %collective-permute-start.9 = (bf16[128,1024]{1,0:T(8,128)(2,1)S(1)}, bf16[128,1024]{1,0:T(8,128)(2,1)S(1)}, u32[]{:S(2)}, u32[]{:S(2)}) collective-permute-start(bf16[128,1024]{1,0:T(8,128)(2,1)S(1)} %get-tuple-element.18), channel_id=1, source_target_pairs={{0,385},{1,386},{2,387},{3,388},{4,389},{5,390},{6,391},{7,392},{8... | collective-permute-start | bytes 786440 | tf_op jit(solution)/shard_map/ppermute | solution.py:279
  78.7 21.4 %collective-permute-start.6 = (bf16[128,1024]{1,0:T(8,128)(2,1)S(1)}, bf16[128,1024]{1,0:T(8,128)(2,1)S(1)}, u32[]{:S(2)}, u32[]{:S(2)}) collective-permute-start(bf16[128,1024]{1,0:T(8,128)(2,1)S(1)} %shard_map.75), channel_id=1, source_target_pairs={{0,193},{1,194},{2,195},{3,196},{4,197},{5,198},{6,199},{7,200},{8... | collective-permute-start | bytes 786440 | tf_op jit(solution)/shard_map/ppermute | solution.py:279
  87.1 21.6 %collective-permute-start.4 = (bf16[128,1024]{1,0:T(8,128)(2,1)S(1)}, bf16[128,1024]{1,0:T(8,128)(2,1)S(1)}, u32[]{:S(2)}, u32[]{:S(2)}) collective-permute-start(bf16[128,1024]{1,0:T(8,128)(2,1)S(1)} %shard_map.74), channel_id=1, source_target_pairs={{0,1},{1,2},{2,3},{3,4},{4,5},{5,6},{6,7},{7,8},{8,9},{9,10},{10,1... | collective-permute-start | bytes 786440 | tf_op jit(solution)/shard_map/ppermute | solution.py:279

commit v2 on v1

--- a/solution.py
+++ b/solution.py
@@ -43,30 +43,37 @@
     return pltpu.with_memory_space_constraint(x, pltpu.VMEM)
 
 
+def in_hbm(x):
+    return pltpu.with_memory_space_constraint(x, pltpu.HBM)
+
+
 def frequencies():
     half = HEAD // 2
     freq = THETA ** (-(2.0 * np.arange(half)) / HEAD)
     return np.concatenate([freq, freq]).astype(np.float32)[None]
 
 
-def doc_start(position, lens_ref):
+LENGTHS, NUMERATOR, DENOMINATOR = 3, 7, 8
+
+
+def doc_start(position, scalars):
     end = 0
     start = jnp.zeros_like(position)
     for d in range(4):
-        length = lens_ref[0, d]
+        length = scalars[LENGTHS + d]
         end = end + length
         start = start + jnp.where(position >= end, length, 0)
     return start
 
 
-def rotation(where_ref, lens_ref, num_ref, den_ref, freq_ref, scale):
-    shard = where_ref[0] * 8 + where_ref[1] * 2 + where_ref[2]
+def rotation(scalars, freq_ref, scale):
+    shard = scalars[0] * 8 + scalars[1] * 2 + scalars[2]
     row = lax.broadcasted_iota(jnp.int32, (128, HEAD), 0)
     lane = lax.broadcasted_iota(jnp.int32, (128, HEAD), 1)
     position = jnp.where(row < SPAN, shard * SPAN + row, (63 - shard) * SPAN + row - SPAN)
-    offset = (position - doc_start(position, lens_ref)).astype(jnp.float32)
-    ratio = jnp.full((128, HEAD), num_ref[0], jnp.int32).astype(jnp.float32) / jnp.full(
-        (128, HEAD), den_ref[0], jnp.int32
+    offset = (position - doc_start(position, scalars)).astype(jnp.float32)
+    ratio = jnp.full((128, HEAD), scalars[NUMERATOR], jnp.int32).astype(jnp.float32) / jnp.full(
+        (128, HEAD), scalars[DENOMINATOR], jnp.int32
     ).astype(jnp.float32)
     angle = offset * ratio * freq_ref[...]
     cosine = jnp.cos(angle) * scale
@@ -79,38 +86,40 @@
     return (wide * cosine + pltpu.roll(wide, HEAD // 2, 1) * sine).astype(jnp.bfloat16)
 
 
-def pack_keys_kernel(where_ref, lens_ref, num_ref, den_ref, freq_ref, k_ref, v_ref, kv_ref):
-    cosine, sine = rotation(where_ref, lens_ref, num_ref, den_ref, freq_ref, 1.0)
+def pack_keys_kernel(scalars, freq_ref, k_ref, v_ref, kv_ref):
+    cosine, sine = rotation(scalars, freq_ref, 1.0)
     for h in range(KV_HEADS):
         cols = slice(h * HEAD, (h + 1) * HEAD)
         kv_ref[h, :, :HEAD] = turn(k_ref[:, cols], cosine, sine)
         kv_ref[h, :, HEAD:] = v_ref[:, cols].T
 
 
-def pack_queries_kernel(where_ref, lens_ref, num_ref, den_ref, freq_ref, q_ref, *q_out):
-    cosine, sine = rotation(where_ref, lens_ref, num_ref, den_ref, freq_ref, QUERY_SCALE)
+def pack_queries_kernel(scalars, freq_ref, q_ref, *q_out):
+    cosine, sine = rotation(scalars, freq_ref, QUERY_SCALE)
     for d in range(4):
-        group = lax.rem(where_ref[0] + d, 4)
+        group = lax.rem(scalars[0] + d, 4)
         for h in range(GROUP):
             start = pl.multiple_of(group * (GROUP * HEAD) + h * HEAD, HEAD)
             q_out[d][:, h * HEAD : (h + 1) * HEAD] = turn(q_ref[:, pl.ds(start, HEAD)], cosine, sine)
 
 
-def gather_keys(where_ref, blocks, k_ref, vt_ref):
-    yh, core = where_ref[1], where_ref[2]
+def gather_keys(scalars, blocks, k_ref, vt_ref):
+    yh, core = scalars[1], scalars[2]
     sides = (0, 2 * core - 1, 1 - 2 * core, 2)
-    for block, side in zip(blocks, sides):
+    for (mine, others), side in zip(blocks, sides):
         y = lax.rem(yh + side + 4, 4)
         for x in range(4):
             early = pl.multiple_of((x * 8 + y * 2) * SPAN, 2 * SPAN)
             late = pl.multiple_of((62 - x * 8 - y * 2) * SPAN, 2 * SPAN)
+            m, o = mine[x], others[x]
+            zero, one = jnp.where(core == 0, m, o), jnp.where(core == 0, o, m)
             k_ref[pl.ds(early, 2 * SPAN), :] = jnp.concatenate(
-                [block[0, x, :SPAN, :HEAD], block[1, x, :SPAN, :HEAD]], axis=0
+                [zero[:SPAN, :HEAD], one[:SPAN, :HEAD]], axis=0
             )
             k_ref[pl.ds(late, 2 * SPAN), :] = jnp.concatenate(
-                [block[1, x, SPAN:, :HEAD], block[0, x, SPAN:, :HEAD]], axis=0
-            )
-            a, b = block[0, x, :, HEAD:], block[1, x, :, HEAD:]
+                [one[SPAN:, :HEAD], zero[SPAN:, :HEAD]], axis=0
+            )
+            a, b = zero[:, HEAD:], one[:, HEAD:]
             vt_ref[:HEAD, pl.ds(early, 2 * SPAN)] = jnp.concatenate([a[:, :SPAN], b[:, :SPAN]], axis=1)
             vt_ref[:HEAD, pl.ds(late, 2 * SPAN)] = jnp.concatenate([b[:, SPAN:], a[:, SPAN:]], axis=1)
     k_ref[TOKENS:, :] = jnp.zeros((TILE, HEAD), jnp.bfloat16)
@@ -118,8 +127,8 @@
     vt_ref[HEAD:, :] = jnp.ones((SUMS, TOKENS + TILE), jnp.bfloat16)
 
 
-def attend_block(where_ref, lens_ref, dx, q_ref, k_ref, vt_ref, o_ref, s_scr, m_scr, acc_scr):
-    shard = lax.rem(where_ref[0] - dx + 4, 4) * 8 + where_ref[1] * 2 + where_ref[2]
+def attend_block(scalars, dx, q_ref, k_ref, vt_ref, o_ref, s_scr, m_scr, acc_scr):
+    shard = lax.rem(scalars[0] - dx + 4, 4) * 8 + scalars[1] * 2 + scalars[2]
     width = GROUP * SPAN
     key = lax.broadcasted_iota(jnp.int32, (TILE, HEAD), 0)
     token = lax.rem(lax.broadcasted_iota(jnp.int32, (8, HEAD), 1), SPAN)
@@ -128,13 +137,13 @@
         rows = pl.ds(pl.multiple_of(half * SPAN, SPAN), SPAN)
         block = jnp.where(half == 0, shard, 63 - shard)
         first = block * SPAN
-        low = lax.div(doc_start(first, lens_ref), HEAD) * HEAD
+        low = lax.div(doc_start(first, scalars), HEAD) * HEAD
         count = lax.div(first - low, TILE) + 1
         q_tile = jnp.concatenate(
             [q_ref[rows, h * HEAD : (h + 1) * HEAD] for h in range(GROUP)], axis=0
         )
         q_pos = first + token
-        q_start = doc_start(q_pos, lens_ref)
+        q_start = doc_start(q_pos, scalars)
         m_scr[...] = jnp.full(m_scr.shape, MASKED, jnp.float32)
         acc_scr[...] = jnp.zeros_like(acc_scr)
 
@@ -175,13 +184,14 @@
     lax.fori_loop(0, 2, one_half, 0)
 
 
-def first_kernel(dx, where_ref, lens_ref, q_ref, b0, b1, b2, b3, o_ref, k_ref, vt_ref, *scratch):
-    gather_keys(where_ref, (b0, b1, b2, b3), k_ref, vt_ref)
-    attend_block(where_ref, lens_ref, dx, q_ref, k_ref, vt_ref, o_ref, *scratch)
-
-
-def next_kernel(dx, where_ref, lens_ref, q_ref, k_ref, vt_ref, o_ref, *scratch):
-    attend_block(where_ref, lens_ref, dx, q_ref, k_ref, vt_ref, o_ref, *scratch)
+def first_kernel(dx, scalars, q_ref, *refs):
+    halves, (o_ref, k_ref, vt_ref), scratch = refs[:8], refs[8:11], refs[11:]
+    gather_keys(scalars, [halves[i : i + 2] for i in range(0, 8, 2)], k_ref, vt_ref)
+    attend_block(scalars, dx, q_ref, k_ref, vt_ref, o_ref, *scratch)
+
+
+def next_kernel(dx, scalars, q_ref, k_ref, vt_ref, o_ref, *scratch):
+    attend_block(scalars, dx, q_ref, k_ref, vt_ref, o_ref, *scratch)
 
 
 def first_place_kernel(col_ref, piece_ref, out_ref):
@@ -212,40 +222,44 @@
 
 def layer(queries, keys, values, doc_lengths, interp_num, interp_den):
     bf16 = jnp.bfloat16
-    where = jnp.stack([lax.axis_index(a) for a in ("x", "yh", "c")]).astype(jnp.int32)
+    place_in = jnp.stack([lax.axis_index(a) for a in ("x", "yh", "c")]).astype(jnp.int32)
+    scalars = jnp.concatenate([place_in, doc_lengths[0], interp_num, interp_den])
     smem = pl.BlockSpec(memory_space=pltpu.SMEM)
     vmem = pl.BlockSpec(memory_space=pltpu.VMEM)
     piece = pltpu.VMEM((128, GROUP * HEAD), bf16)
-    turning = (where, doc_lengths, interp_num, interp_den, frequencies())
+    freq = in_hbm(jnp.asarray(frequencies()))
     kv = pl.pallas_call(
         pack_keys_kernel,
         out_shape=pltpu.VMEM((4, 128, 2 * HEAD), bf16),
-        in_specs=[smem] * 4 + [vmem] * 3,
+        in_specs=[smem] + [vmem] * 3,
         out_specs=vmem,
         name="pack_keys",
         compiler_params=room(12),
-    )(*turning, keys[0], values[0])
+    )(scalars, freq, in_hbm(keys[0]), in_hbm(values[0]))
     packed = pl.pallas_call(
         pack_queries_kernel,
         out_shape=(piece,) * 4,
-        in_specs=[smem] * 4 + [vmem] * 2,
+        in_specs=[smem] + [vmem] * 2,
         out_specs=(vmem,) * 4,
         name="pack_queries",
         compiler_params=room(12),
-    )(*turning, queries[0])
-    kv = lax.all_to_all(kv, "x", 0, 0, tiled=True)
-    near = lax.all_gather(kv, "c", axis=0)
+    )(scalars, freq, queries[0])
+    mine = lax.all_to_all(kv, "x", 0, 0, tiled=True)
+    swap_cores = functools.partial(lax.ppermute, axis_name="c", perm=[(0, 1), (1, 0)])
     ring = [(y * 2 + c, (y + 1 - 2 * c) % 4 * 2 + c) for y in range(4) for c in range(2)]
-    one_on = lax.ppermute(near, ("yh", "c"), ring)
-    core = lax.axis_index("c")
-    half = lax.dynamic_index_in_dim(one_on, core, 0, keepdims=False)
-    two_on = lax.ppermute(half, ("yh", "c"), ring)
-    other = lax.ppermute(one_on, "c", [(0, 1), (1, 0)])
-    far = lax.all_gather(two_on, "c", axis=0)
+    pass_on = functools.partial(lax.ppermute, axis_name=("yh", "c"), perm=ring)
+    near_mine = pass_on(mine)
+    twin = swap_cores(mine)
+    near_twin = pass_on(twin)
+    far_mine = pass_on(near_mine)
+    other_a = swap_cores(near_mine)
+    other_b = swap_cores(near_twin)
+    far_twin = swap_cores(far_mine)
+    halves = (mine, twin, near_mine, near_twin, other_b, other_a, far_mine, far_twin)
     moved = {0: packed[0]}
     for d in (2, 1, 3):
         moved[d] = lax.ppermute(packed[d], AXES, route(d, 0))
-    lengths = jnp.minimum(doc_lengths, TOKENS)
+    marked = jnp.minimum(scalars, TOKENS)
     scratch = [
         pltpu.VMEM((ROUNDS, TILE, GROUP * SPAN), jnp.float32),
         pltpu.VMEM((8, GROUP * SPAN), jnp.float32),
@@ -262,24 +276,24 @@
             result, *ordered = pl.pallas_call(
                 functools.partial(first_kernel, d),
                 out_shape=(piece,) + laid_out,
-                in_specs=[smem] * 2 + [vmem] * 5,
+                in_specs=[smem] + [vmem] * 9,
                 out_specs=(vmem,) * 3,
                 scratch_shapes=scratch,
                 compiler_params=room(24),
-            )(where, lengths, *map(held, (moved[d], near, one_on, other, far)))
+            )(marked, *map(held, (moved[d], *halves)))
         else:
             result = pl.pallas_call(
                 functools.partial(next_kernel, d),
                 out_shape=piece,
-                in_specs=[smem] * 2 + [vmem] * 3,
+                in_specs=[smem] + [vmem] * 3,
                 out_specs=vmem,
                 scratch_shapes=scratch,
                 compiler_params=room(24),
-            )(where, lengths, *map(held, (moved[d], *ordered)))
+            )(marked, *map(held, (moved[d], *ordered)))
         handed[d] = lax.ppermute(result, AXES, route(-d, 1))
     out = None
     for d in (2, 1, 3, 0):
-        out = place(handed[d], out, (where[:1] + d) % 4)
+        out = place(handed[d], out, (marked[:1] + d) % 4)
     return out
 
 

time: 110 us -> 103 us (0.936)
  starting transfers between devices: 33.5 us -> 57.4 us
  waiting for transfers between devices: 26.4 us -> 11.5 us
  blocking collectives: 24 us -> 10.2 us
  local copies, waits for them, and re-layouts: 3.16 us -> 0.73 us
    ppermute x3 -> x7, starting transfers between devices: 9.63 us -> 34.8 us  [the longest x1 7.3 us: layer(): twin = swap_cores(mine)]
    all_gather x2 -> x0, blocking collectives: 13.8 us -> none  [the longest x1 11.2 us: layer(): near = lax.all_gather(kv, 'c', axis=0)]
    ppermute x3 -> x7, waiting for transfers between devices: 9.82 us -> 0.02 us  [the longest x1 0.01 us: layer(): far_mine = pass_on(near_mine)]
    ppermute x4, waiting for transfers between devices: 16.1 us -> 11.5 us  [layer(): handed[d] = lax.ppermute(result, AXES, route(-d, 1))]
    unnamed x14 -> x2, local copies, waits for them, and re-layouts: 3.13 us -> 0.01 us
    ppermute x4, starting transfers between devices: 15 us -> 13.6 us  [layer(): handed[d] = lax.ppermute(result, AXES, route(-d, 1))]
  transfers between devices with their start and end apart: 10 -> 14, of which waited for: 5 -> 3; matrix products, arithmetic and copies ran while one was open for 0% -> 0% of each run, Pallas kernels for 17% -> 18%
where the time goes in v2:
time: 103 us
  starting transfers between devices  57.4 us (56%)
  Pallas kernels  21.1 us (20%)
  waiting for transfers between devices  11.5 us (11%)
  blocking collectives  10.2 us (10%)
  between operations  1.9 us (2%)
    ppermute x4, starting transfers between devices, layer(): handed[d] = lax.ppermute(result, AXES, route(-d, 1))  13.6 us
    ppermute x4, waiting for transfers between devices, layer(): handed[d] = lax.ppermute(result, AXES, route(-d, 1))  11.5 us
    pallas_call x3, Pallas kernels, layer(): pl.pallas_call(functools.partial(next_kernel, d), out_shape=piece, in_spe...  10.2 us
    all_to_all x1, blocking collectives, layer(): mine = lax.all_to_all(kv, 'x', 0, 0, tiled=True)  10.2 us
    ppermute x3, starting transfers between devices, layer(): moved[d] = lax.ppermute(packed[d], AXES, route(d, 0))  9.08 us
    ppermute x1, starting transfers between devices, layer(): twin = swap_cores(mine)  7.3 us
    ppermute x1, starting transfers between devices, layer(): near_mine = pass_on(mine)  5.9 us
    ppermute x1, starting transfers between devices, layer(): far_mine = pass_on(near_mine)  5.75 us
  transfers between devices with their start and end apart: 14, of which 3 were waited for; matrix products, arithmetic and copies ran while one was open for 0% of the time, Pallas kernels for 18%

profile of v2, /device:TPU:1, one launch (start us, length us, event | category | flops | bytes accessed | tf_op | source)
XLA Modules:
  0.0 102.8 jit_solution(2684970972660856138)
XLA Ops:
  1.4 0.7 concatenate.3.scalars
  2.1 1.4 %pack_keys.1 = bf16[4,128,256]{2,1,0:T(8,128)(2,1)S(1)} custom-call(s32[9]{0:T(128)S(1)} %concatenate.3.scalars, f32[1,128]{1,0:T(1,128)} %constant.62.clone.freq_ref, bf16[128,512]{1,0:T(8,128)(2,1)} %bitcast.15, bf16[128,512]{1,0:T(8,128)(2,1)} %bitcast.16), custom_call_target="tpu_custom_call" | custom-call | tf_op jit(solution)/shard_map/pack_keys/pallas_call | solution.py:231
  3.5 10.2 %all_to_all.5.refs_0_ = bf16[4,128,256]{2,1,0:T(8,128)(2,1)S(1)} all-to-all(bf16[4,128,256]{2,1,0:T(8,128)(2,1)S(1)} %pack_keys.1), channel_id=1, replica_groups=mesh['x'=4,'yh'=4,'c'=2,'yl'=2,'z'=12] {'x'}, dimensions={0} | all-to-all | bytes 524288 | tf_op jit(solution)/shard_map/all_to_all | solution.py:247
  13.6 5.9 %collective-permute-start.2 = (bf16[4,128,256]{2,1,0:T(8,128)(2,1)S(1)}, bf16[4,128,256]{2,1,0:T(8,128)(2,1)S(1)}, u32[]{:S(2)}, u32[]{:S(2)}) collective-permute-start(bf16[4,128,256]{2,1,0:T(8,128)(2,1)S(1)} %all_to_all.5.refs_0_), channel_id=1, source_target_pairs={{0,48},{24,168},{48,96},{72,24},{96,144},{120,72},{144,0},{168,120... | collective-permute-start | bytes 786440 | tf_op jit(solution)/shard_map/ppermute | solution.py:251
  19.6 7.3 %collective-permute-start.1 = (bf16[4,128,256]{2,1,0:T(8,128)(2,1)S(1)}, bf16[4,128,256]{2,1,0:T(8,128)(2,1)S(1)}, u32[]{:S(2)}, u32[]{:S(2)}) collective-permute-start(bf16[4,128,256]{2,1,0:T(8,128)(2,1)S(1)} %all_to_all.5.refs_0_), channel_id=1, source_target_pairs={{0,24},{24,0},{1,25},{25,1},{2,26},{26,2},{3,27},{27,3},{4,28},{28... | collective-permute-start | bytes 786440 | tf_op jit(solution)/shard_map/ppermute | solution.py:252
  26.9 5.8 %collective-permute-start.6 = (bf16[4,128,256]{2,1,0:T(8,128)(2,1)S(1)}, bf16[4,128,256]{2,1,0:T(8,128)(2,1)S(1)}, u32[]{:S(2)}, u32[]{:S(2)}) collective-permute-start(bf16[4,128,256]{2,1,0:T(8,128)(2,1)S(1)} %collective-permute-done.2.refs_2_), channel_id=1, source_target_pairs={{0,48},{24,168},{48,96},{72,24},{96,144},{120,72},{144,0},{168,120... | collective-permute-start | bytes 786440 | tf_op jit(solution)/shard_map/ppermute | solution.py:254
  32.6 1.9 %collective-permute-start.3 = (bf16[4,128,256]{2,1,0:T(8,128)(2,1)S(1)}, bf16[4,128,256]{2,1,0:T(8,128)(2,1)S(1)}, u32[]{:S(2)}, u32[]{:S(2)}) collective-permute-start(bf16[4,128,256]{2,1,0:T(8,128)(2,1)S(1)} %collective-permute-done.1.refs_1_), channel_id=1, source_target_pairs={{0,48},{24,168},{48,96},{72,24},{96,144},{120,72},{144,0},{168,120... | collective-permute-start | bytes 786440 | tf_op jit(solution)/shard_map/ppermute | solution.py:253
  34.6 1.5 %pack_queries.1 = (bf16[128,1024]{1,0:T(8,128)(2,1)S(1)}, bf16[128,1024]{1,0:T(8,128)(2,1)S(1)}, bf16[128,1024]{1,0:T(8,128)(2,1)S(1)}, bf16[128,1024]{1,0:T(8,128)(2,1)S(1)}) custom-call(s32[9]{0:T(128)S(1)} %concatenate.3.scalars, f32[1,128]{1,0:T(1,128)} %constant.62.clone.freq_ref, bf16[128,4096]{1,0:T(8,128)(2,1)S(1)} %bitcast.8), custom_call_target="tpu_custom_call" | custom-call | tf_op jit(solution)/shard_map/pack_queries/pallas_call | solution.py:239
  36.1 2.6 %collective-permute-start = (bf16[128,1024]{1,0:T(8,128)(2,1)S(1)}, bf16[128,1024]{1,0:T(8,128)(2,1)S(1)}, u32[]{:S(2)}, u32[]{:S(2)}) collective-permute-start(bf16[128,1024]{1,0:T(8,128)(2,1)S(1)} %get-tuple-element.13), channel_id=1, source_target_pairs={{0,384},{1,385},{2,386},{3,387},{4,388},{5,389},{6,390},{7,391},{8... | collective-permute-start | bytes 786440 | tf_op jit(solution)/shard_map/ppermute | solution.py:261
  38.7 5.4 %collective-permute-start.5 = (bf16[4,128,256]{2,1,0:T(8,128)(2,1)S(1)}, bf16[4,128,256]{2,1,0:T(8,128)(2,1)S(1)}, u32[]{:S(2)}, u32[]{:S(2)}) collective-permute-start(bf16[4,128,256]{2,1,0:T(8,128)(2,1)S(1)} %collective-permute-done.2.refs_2_), channel_id=1, source_target_pairs={{0,24},{24,0},{1,25},{25,1},{2,26},{26,2},{3,27},{27,3},{4,28},{28... | collective-permute-start | bytes 786440 | tf_op jit(solution)/shard_map/ppermute | solution.py:255
  44.1 5.7 %collective-permute-start.7 = (bf16[4,128,256]{2,1,0:T(8,128)(2,1)S(1)}, bf16[4,128,256]{2,1,0:T(8,128)(2,1)S(1)}, u32[]{:S(2)}, u32[]{:S(2)}) collective-permute-start(bf16[4,128,256]{2,1,0:T(8,128)(2,1)S(1)} %collective-permute-done.6.refs_6_), channel_id=1, source_target_pairs={{0,24},{24,0},{1,25},{25,1},{2,26},{26,2},{3,27},{27,3},{4,28},{28... | collective-permute-start | bytes 786440 | tf_op jit(solution)/shard_map/ppermute | solution.py:257
  49.9 2.8 %collective-permute-start.4 = (bf16[4,128,256]{2,1,0:T(8,128)(2,1)S(1)}, bf16[4,128,256]{2,1,0:T(8,128)(2,1)S(1)}, u32[]{:S(2)}, u32[]{:S(2)}) collective-permute-start(bf16[4,128,256]{2,1,0:T(8,128)(2,1)S(1)} %collective-permute-done.3.refs_3_), channel_id=1, source_target_pairs={{0,24},{24,0},{1,25},{25,1},{2,26},{26,2},{3,27},{27,3},{4,28},{28... | collective-permute-start | bytes 786440 | tf_op jit(solution)/shard_map/ppermute | solution.py:256
  52.7 2.2 %collective-permute-start.11 = (bf16[128,1024]{1,0:T(8,128)(2,1)S(1)}, bf16[128,1024]{1,0:T(8,128)(2,1)S(1)}, u32[]{:S(2)}, u32[]{:S(2)}) collective-permute-start(bf16[128,1024]{1,0:T(8,128)(2,1)S(1)} %get-tuple-element.17), channel_id=1, source_target_pairs={{0,192},{1,193},{2,194},{3,195},{4,196},{5,197},{6,198},{7,199},{8... | collective-permute-start | bytes 786440 | tf_op jit(solution)/shard_map/ppermute | solution.py:261
  54.9 4.3 %collective-permute-start.9 = (bf16[128,1024]{1,0:T(8,128)(2,1)S(1)}, bf16[128,1024]{1,0:T(8,128)(2,1)S(1)}, u32[]{:S(2)}, u32[]{:S(2)}) collective-permute-start(bf16[128,1024]{1,0:T(8,128)(2,1)S(1)} %get-tuple-element.16), channel_id=1, source_target_pairs={{0,576},{1,577},{2,578},{3,579},{4,580},{5,581},{6,582},{7,583},{8... | collective-permute-start | bytes 786440 | tf_op jit(solution)/shard_map/ppermute | solution.py:261
  59.2 5.1 %shard_map.73 = (bf16[128,1024]{1,0:T(8,128)(2,1)S(1)}, bf16[4608,128]{1,0:T(8,128)(2,1)S(1)}, bf16[144,4608]{1,0:T(8,128)(2,1)S(1)}) custom-call(s32[9]{0:T(128)S(1)} %broadcast_minimum_fusion.scalars, bf16[128,1024]{1,0:T(8,128)(2,1)S(1)} %collective-permute-done.q_ref, bf16[4,128,256]{2,1,0:T(8,128)(2,1)S(1)} %all_to_all.5.refs_0_, ...), custom_call_target="tpu_custom_call" | custom-call | tf_op jit(solution)/shard_map/pallas_call | solution.py:276
  64.3 4.7 %shard_map.76 = bf16[128,1024]{1,0:T(8,128)(2,1)S(1)} custom-call(s32[9]{0:T(128)S(1)} %broadcast_minimum_fusion.scalars, bf16[128,1024]{1,0:T(8,128)(2,1)S(1)} %collective-permute-done.11.q_ref, bf16[4608,128]{1,0:T(8,128)(2,1)S(1)} %get-tuple-element.14.k_ref, bf16[144,4608]{1,0:T(8,128)(2,1)S(1)} %get-tuple-element.15.vt_ref), custom_call_target="tpu_custom_call" | custom-call | tf_op jit(solution)/shard_map/pallas_call | solution.py:285
  69.0 1.9 %collective-permute-start.12 = (bf16[128,1024]{1,0:T(8,128)(2,1)S(1)}, bf16[128,1024]{1,0:T(8,128)(2,1)S(1)}, u32[]{:S(2)}, u32[]{:S(2)}) collective-permute-start(bf16[128,1024]{1,0:T(8,128)(2,1)S(1)} %shard_map.76), channel_id=1, source_target_pairs={{0,577},{1,578},{2,579},{3,580},{4,581},{5,582},{6,583},{7,584},{8... | collective-permute-start | bytes 786440 | tf_op jit(solution)/shard_map/ppermute | solution.py:293
  70.9 2.7 %collective-permute-start.13 = (bf16[128,1024]{1,0:T(8,128)(2,1)S(1)}, bf16[128,1024]{1,0:T(8,128)(2,1)S(1)}, u32[]{:S(2)}, u32[]{:S(2)}) collective-permute-start(bf16[128,1024]{1,0:T(8,128)(2,1)S(1)} %get-tuple-element.18), channel_id=1, source_target_pairs={{0,385},{1,386},{2,387},{3,388},{4,389},{5,390},{6,391},{7,392},{8... | collective-permute-start | bytes 786440 | tf_op jit(solution)/shard_map/ppermute | solution.py:293
  73.6 2.8 %shard_map.75 = bf16[128,1024]{1,0:T(8,128)(2,1)S(1)} custom-call(s32[9]{0:T(128)S(1)} %broadcast_minimum_fusion.scalars, bf16[128,1024]{1,0:T(8,128)(2,1)S(1)} %collective-permute-done.9.q_ref, bf16[4608,128]{1,0:T(8,128)(2,1)S(1)} %get-tuple-element.14.k_ref, bf16[144,4608]{1,0:T(8,128)(2,1)S(1)} %get-tuple-element.15.vt_ref), custom_call_target="tpu_custom_call" | custom-call | tf_op jit(solution)/shard_map/pallas_call | solution.py:285
  76.4 5.6 %collective-permute-start.10 = (bf16[128,1024]{1,0:T(8,128)(2,1)S(1)}, bf16[128,1024]{1,0:T(8,128)(2,1)S(1)}, u32[]{:S(2)}, u32[]{:S(2)}) collective-permute-start(bf16[128,1024]{1,0:T(8,128)(2,1)S(1)} %shard_map.75), channel_id=1, source_target_pairs={{0,193},{1,194},{2,195},{3,196},{4,197},{5,198},{6,199},{7,200},{8... | collective-permute-start | bytes 786440 | tf_op jit(solution)/shard_map/ppermute | solution.py:293
  82.0 2.8 %shard_map.74 = bf16[128,1024]{1,0:T(8,128)(2,1)S(1)} custom-call(s32[9]{0:T(128)S(1)} %broadcast_minimum_fusion.scalars, bf16[128,1024]{1,0:T(8,128)(2,1)S(1)} %get-tuple-element.12.q_ref, bf16[4608,128]{1,0:T(8,128)(2,1)S(1)} %get-tuple-element.14.k_ref, bf16[144,4608]{1,0:T(8,128)(2,1)S(1)} %get-tuple-element.15.vt_ref), custom_call_target="tpu_custom_call" | custom-call | tf_op jit(solution)/shard_map/pallas_call | solution.py:285
  84.8 3.4 %collective-permute-start.8 = (bf16[128,1024]{1,0:T(8,128)(2,1)S(1)}, bf16[128,1024]{1,0:T(8,128)(2,1)S(1)}, u32[]{:S(2)}, u32[]{:S(2)}) collective-permute-start(bf16[128,1024]{1,0:T(8,128)(2,1)S(1)} %shard_map.74), channel_id=1, source_target_pairs={{0,1},{1,2},{2,3},{3,4},{4,5},{5,6},{6,7},{7,8},{8,9},{9,10},{10,1... | collective-permute-start | bytes 786440 | tf_op jit(solution)/shard_map/ppermute | solution.py:293
  90.3 5.1 %collective-permute-done.10.piece_ref = bf16[128,1024]{1,0:T(8,128)(2,1)S(1)} collective-permute-done((bf16[128,1024]{1,0:T(8,128)(2,1)S(1)}, bf16[128,1024]{1,0:T(8,128)(2,1)S(1)}, u32[]{:S(2)}, u32[]{:S(2)}) %collective-permute-start.10) | collective-permute-done | bytes 262176 | tf_op jit(solution)/shard_map/ppermute | solution.py:293
  96.2 5.8 %collective-permute-done.8.piece_ref = bf16[128,1024]{1,0:T(8,128)(2,1)S(1)} collective-permute-done((bf16[128,1024]{1,0:T(8,128)(2,1)S(1)}, bf16[128,1024]{1,0:T(8,128)(2,1)S(1)}, u32[]{:S(2)}, u32[]{:S(2)}) %collective-permute-start.8) | collective-permute-done | bytes 262176 | tf_op jit(solution)/shard_map/ppermute | solution.py:293
  (19 shorter events, 3.4 us)
Async XLA Ops:
  0.0 34.6 %copy-start = (bf16[1,128,4096]{2,1,0:T(8,128)(2,1)S(1)}, bf16[1,128,4096]{2,1,0:T(8,128)(2,1)}, u32[]{:S(2)}) copy-start(bf16[1,128,4096]{2,1,0:T(8,128)(2,1)} %param.7) | copy-start | bytes 3145732
  13.6 13.2 %collective-permute-start.2 = (bf16[4,128,256]{2,1,0:T(8,128)(2,1)S(1)}, bf16[4,128,256]{2,1,0:T(8,128)(2,1)S(1)}, u32[]{:S(2)}, u32[]{:S(2)}) collective-permute-start(bf16[4,128,256]{2,1,0:T(8,128)(2,1)S(1)} %all_to_all.5.refs_0_), channel_id=1, source_target_pairs={{0,48},{24,168},{48,96},{72,24},{96,144},{120,72},{144,0},{168,120... | collective-permute-start | bytes 786440 | tf_op jit(solution)/shard_map/ppermute | solution.py:251
  19.6 13.1 %collective-permute-start.1 = (bf16[4,128,256]{2,1,0:T(8,128)(2,1)S(1)}, bf16[4,128,256]{2,1,0:T(8,128)(2,1)S(1)}, u32[]{:S(2)}, u32[]{:S(2)}) collective-permute-start(bf16[4,128,256]{2,1,0:T(8,128)(2,1)S(1)} %all_to_all.5.refs_0_), channel_id=1, source_target_pairs={{0,24},{24,0},{1,25},{25,1},{2,26},{26,2},{3,27},{27,3},{4,28},{28... | collective-permute-start | bytes 786440 | tf_op jit(solution)/shard_map/ppermute | solution.py:252
  26.9 17.3 %collective-permute-start.6 = (bf16[4,128,256]{2,1,0:T(8,128)(2,1)S(1)}, bf16[4,128,256]{2,1,0:T(8,128)(2,1)S(1)}, u32[]{:S(2)}, u32[]{:S(2)}) collective-permute-start(bf16[4,128,256]{2,1,0:T(8,128)(2,1)S(1)} %collective-permute-done.2.refs_2_), channel_id=1, source_target_pairs={{0,48},{24,168},{48,96},{72,24},{96,144},{120,72},{144,0},{168,120... | collective-permute-start | bytes 786440 | tf_op jit(solution)/shard_map/ppermute | solution.py:254
  32.6 17.2 %collective-permute-start.3 = (bf16[4,128,256]{2,1,0:T(8,128)(2,1)S(1)}, bf16[4,128,256]{2,1,0:T(8,128)(2,1)S(1)}, u32[]{:S(2)}, u32[]{:S(2)}) collective-permute-start(bf16[4,128,256]{2,1,0:T(8,128)(2,1)S(1)} %collective-permute-done.1.refs_1_), channel_id=1, source_target_pairs={{0,48},{24,168},{48,96},{72,24},{96,144},{120,72},{144,0},{168,120... | collective-permute-start | bytes 786440 | tf_op jit(solution)/shard_map/ppermute | solution.py:253
  36.1 18.7 %collective-permute-start = (bf16[128,1024]{1,0:T(8,128)(2,1)S(1)}, bf16[128,1024]{1,0:T(8,128)(2,1)S(1)}, u32[]{:S(2)}, u32[]{:S(2)}) collective-permute-start(bf16[128,1024]{1,0:T(8,128)(2,1)S(1)} %get-tuple-element.13), channel_id=1, source_target_pairs={{0,384},{1,385},{2,386},{3,387},{4,388},{5,389},{6,390},{7,391},{8... | collective-permute-start | bytes 786440 | tf_op jit(solution)/shard_map/ppermute | solution.py:261
  38.7 20.5 %collective-permute-start.5 = (bf16[4,128,256]{2,1,0:T(8,128)(2,1)S(1)}, bf16[4,128,256]{2,1,0:T(8,128)(2,1)S(1)}, u32[]{:S(2)}, u32[]{:S(2)}) collective-permute-start(bf16[4,128,256]{2,1,0:T(8,128)(2,1)S(1)} %collective-permute-done.2.refs_2_), channel_id=1, source_target_pairs={{0,24},{24,0},{1,25},{25,1},{2,26},{26,2},{3,27},{27,3},{4,28},{28... | collective-permute-start | bytes 786440 | tf_op jit(solution)/shard_map/ppermute | solution.py:255
  44.1 15.1 %collective-permute-start.7 = (bf16[4,128,256]{2,1,0:T(8,128)(2,1)S(1)}, bf16[4,128,256]{2,1,0:T(8,128)(2,1)S(1)}, u32[]{:S(2)}, u32[]{:S(2)}) collective-permute-start(bf16[4,128,256]{2,1,0:T(8,128)(2,1)S(1)} %collective-permute-done.6.refs_6_), channel_id=1, source_target_pairs={{0,24},{24,0},{1,25},{25,1},{2,26},{26,2},{3,27},{27,3},{4,28},{28... | collective-permute-start | bytes 786440 | tf_op jit(solution)/shard_map/ppermute | solution.py:257
  49.9 9.4 %collective-permute-start.4 = (bf16[4,128,256]{2,1,0:T(8,128)(2,1)S(1)}, bf16[4,128,256]{2,1,0:T(8,128)(2,1)S(1)}, u32[]{:S(2)}, u32[]{:S(2)}) collective-permute-start(bf16[4,128,256]{2,1,0:T(8,128)(2,1)S(1)} %collective-permute-done.3.refs_3_), channel_id=1, source_target_pairs={{0,24},{24,0},{1,25},{25,1},{2,26},{26,2},{3,27},{27,3},{4,28},{28... | collective-permute-start | bytes 786440 | tf_op jit(solution)/shard_map/ppermute | solution.py:256
  52.7 11.6 %collective-permute-start.11 = (bf16[128,1024]{1,0:T(8,128)(2,1)S(1)}, bf16[128,1024]{1,0:T(8,128)(2,1)S(1)}, u32[]{:S(2)}, u32[]{:S(2)}) collective-permute-start(bf16[128,1024]{1,0:T(8,128)(2,1)S(1)} %get-tuple-element.17), channel_id=1, source_target_pairs={{0,192},{1,193},{2,194},{3,195},{4,196},{5,197},{6,198},{7,199},{8... | collective-permute-start | bytes 786440 | tf_op jit(solution)/shard_map/ppermute | solution.py:261
  54.9 18.8 %collective-permute-start.9 = (bf16[128,1024]{1,0:T(8,128)(2,1)S(1)}, bf16[128,1024]{1,0:T(8,128)(2,1)S(1)}, u32[]{:S(2)}, u32[]{:S(2)}) collective-permute-start(bf16[128,1024]{1,0:T(8,128)(2,1)S(1)} %get-tuple-element.16), channel_id=1, source_target_pairs={{0,576},{1,577},{2,578},{3,579},{4,580},{5,581},{6,582},{7,583},{8... | collective-permute-start | bytes 786440 | tf_op jit(solution)/shard_map/ppermute | solution.py:261
  69.0 20.6 %collective-permute-start.12 = (bf16[128,1024]{1,0:T(8,128)(2,1)S(1)}, bf16[128,1024]{1,0:T(8,128)(2,1)S(1)}, u32[]{:S(2)}, u32[]{:S(2)}) collective-permute-start(bf16[128,1024]{1,0:T(8,128)(2,1)S(1)} %shard_map.76), channel_id=1, source_target_pairs={{0,577},{1,578},{2,579},{3,580},{4,581},{5,582},{6,583},{7,584},{8... | collective-permute-start | bytes 786440 | tf_op jit(solution)/shard_map/ppermute | solution.py:293
  70.9 18.0 %collective-permute-start.13 = (bf16[128,1024]{1,0:T(8,128)(2,1)S(1)}, bf16[128,1024]{1,0:T(8,128)(2,1)S(1)}, u32[]{:S(2)}, u32[]{:S(2)}) collective-permute-start(bf16[128,1024]{1,0:T(8,128)(2,1)S(1)} %get-tuple-element.18), channel_id=1, source_target_pairs={{0,385},{1,386},{2,387},{3,388},{4,389},{5,390},{6,391},{7,392},{8... | collective-permute-start | bytes 786440 | tf_op jit(solution)/shard_map/ppermute | solution.py:293
  76.4 19.1 %collective-permute-start.10 = (bf16[128,1024]{1,0:T(8,128)(2,1)S(1)}, bf16[128,1024]{1,0:T(8,128)(2,1)S(1)}, u32[]{:S(2)}, u32[]{:S(2)}) collective-permute-start(bf16[128,1024]{1,0:T(8,128)(2,1)S(1)} %shard_map.75), channel_id=1, source_target_pairs={{0,193},{1,194},{2,195},{3,196},{4,197},{5,198},{6,199},{7,200},{8... | collective-permute-start | bytes 786440 | tf_op jit(solution)/shard_map/ppermute | solution.py:293
  84.8 17.3 %collective-permute-start.8 = (bf16[128,1024]{1,0:T(8,128)(2,1)S(1)}, bf16[128,1024]{1,0:T(8,128)(2,1)S(1)}, u32[]{:S(2)}, u32[]{:S(2)}) collective-permute-start(bf16[128,1024]{1,0:T(8,128)(2,1)S(1)} %shard_map.74), channel_id=1, source_target_pairs={{0,1},{1,2},{2,3},{3,4},{4,5},{5,6},{6,7},{7,8},{8,9},{9,10},{10,1... | collective-permute-start | bytes 786440 | tf_op jit(solution)/shard_map/ppermute | solution.py:293

commit v3 on v2

--- a/solution.py
+++ b/solution.py
@@ -17,6 +17,7 @@
 MASKED = -1e30
 SPAN = 64
 TOKENS = 4096
+CALLS = ((2,), (1,), (3,), (0,))
 TILE = 512
 ROUNDS = 2176 // TILE + 1
 SUMS = 16
@@ -147,35 +148,47 @@
         m_scr[...] = jnp.full(m_scr.shape, MASKED, jnp.float32)
         acc_scr[...] = jnp.zeros_like(acc_scr)
 
-        def scores(t, _):
+        def scores(t, tiles):
+            top = m_scr[...]
+            for u in range(tiles):
+                at = pl.multiple_of(low + (t + u) * TILE, HEAD)
+                bias = jnp.where(
+                    (key <= (q_pos - at)[:1]) & (key >= (q_start - at)[:1]), 0.0, MASKED
+                )
+                s = lax.dot_general(
+                    k_ref[pl.ds(at, TILE), :],
+                    q_tile,
+                    (((1,), (1,)), ((), ())),
+                    preferred_element_type=jnp.float32,
+                )
+                s = s + jnp.concatenate([bias] * (width // HEAD), axis=1)
+                s_scr[t + u] = s
+                top = jnp.maximum(top, jnp.max(s.reshape(TILE // 8, 8, width), axis=0))
+            m_scr[...] = top
+
+        def weigh(t, tiles):
+            weights = []
+            for u in range(tiles):
+                s = s_scr[t + u].reshape(TILE // 8, 8, width) - m_scr[...][None]
+                weights.append(jnp.exp2(s).reshape(TILE, width).astype(jnp.bfloat16))
             at = pl.multiple_of(low + t * TILE, HEAD)
-            bias = jnp.where(
-                (key <= (q_pos - at)[:1]) & (key >= (q_start - at)[:1]), 0.0, MASKED
-            )
-            s = lax.dot_general(
-                k_ref[pl.ds(at, TILE), :],
-                q_tile,
-                (((1,), (1,)), ((), ())),
+            acc_scr[...] += jnp.dot(
+                vt_ref[:, pl.ds(at, tiles * TILE)],
+                jnp.concatenate(weights, axis=0),
                 preferred_element_type=jnp.float32,
             )
-            s = s + jnp.concatenate([bias] * (width // HEAD), axis=1)
-            s_scr[t] = s
-            m_scr[...] = jnp.maximum(m_scr[...], jnp.max(s.reshape(TILE // 8, 8, width), axis=0))
-            return 0
-
-        lax.fori_loop(0, count, scores, 0)
+
+        def in_pairs(step):
+            def pair(i, _):
+                step(2 * i, 2)
+                return 0
+
+            lax.fori_loop(0, lax.div(count, 2), pair, 0)
+            pl.when(lax.rem(count, 2) == 1)(lambda: step(count - 1, 1))
+
+        in_pairs(scores)
         m_scr[...] = jnp.broadcast_to(jnp.max(m_scr[...], axis=0, keepdims=True), m_scr.shape)
-
-        def weigh(t, _):
-            at = pl.multiple_of(low + t * TILE, HEAD)
-            s = s_scr[t].reshape(TILE // 8, 8, width) - m_scr[...][None]
-            w = jnp.exp2(s).reshape(TILE, width).astype(jnp.bfloat16)
-            acc_scr[...] += jnp.dot(
-                vt_ref[:, pl.ds(at, TILE)], w, preferred_element_type=jnp.float32
-            )
-            return 0
-
-        lax.fori_loop(0, count, weigh, 0)
+        in_pairs(weigh)
         out = (acc_scr[:HEAD, :] * (1.0 / acc_scr[HEAD : HEAD + 1, :])).T.astype(jnp.bfloat16)
         for h in range(GROUP):
             o_ref[rows, h * HEAD : (h + 1) * HEAD] = out[h * SPAN : (h + 1) * SPAN]
@@ -184,14 +197,19 @@
     lax.fori_loop(0, 2, one_half, 0)
 
 
-def first_kernel(dx, scalars, q_ref, *refs):
-    halves, (o_ref, k_ref, vt_ref), scratch = refs[:8], refs[8:11], refs[11:]
+def first_kernel(dxs, scalars, *refs):
+    n = len(dxs)
+    queries, halves, outs, (k_ref, vt_ref) = refs[:n], refs[n : n + 8], refs[n + 8 : 2 * n + 8], refs[2 * n + 8 : 2 * n + 10]
     gather_keys(scalars, [halves[i : i + 2] for i in range(0, 8, 2)], k_ref, vt_ref)
-    attend_block(scalars, dx, q_ref, k_ref, vt_ref, o_ref, *scratch)
-
-
-def next_kernel(dx, scalars, q_ref, k_ref, vt_ref, o_ref, *scratch):
-    attend_block(scalars, dx, q_ref, k_ref, vt_ref, o_ref, *scratch)
+    for dx, q_ref, o_ref in zip(dxs, queries, outs):
+        attend_block(scalars, dx, q_ref, k_ref, vt_ref, o_ref, *refs[2 * n + 10 :])
+
+
+def next_kernel(dxs, scalars, *refs):
+    n = len(dxs)
+    queries, (k_ref, vt_ref), outs = refs[:n], refs[n : n + 2], refs[n + 2 : 2 * n + 2]
+    for dx, q_ref, o_ref in zip(dxs, queries, outs):
+        attend_block(scalars, dx, q_ref, k_ref, vt_ref, o_ref, *refs[2 * n + 2 :])
 
 
 def first_place_kernel(col_ref, piece_ref, out_ref):
@@ -271,28 +289,31 @@
     )
     handed = {}
     ordered = None
-    for d in (2, 1, 3, 0):
+    for dxs in CALLS:
+        n = len(dxs)
         if ordered is None:
-            result, *ordered = pl.pallas_call(
-                functools.partial(first_kernel, d),
-                out_shape=(piece,) + laid_out,
-                in_specs=[smem] + [vmem] * 9,
-                out_specs=(vmem,) * 3,
+            *results, key_rows, value_columns = pl.pallas_call(
+                functools.partial(first_kernel, dxs),
+                out_shape=(piece,) * n + laid_out,
+                in_specs=[smem] + [vmem] * (n + 8),
+                out_specs=(vmem,) * (n + 2),
                 scratch_shapes=scratch,
                 compiler_params=room(24),
-            )(marked, *map(held, (moved[d], *halves)))
+            )(marked, *map(held, [moved[d] for d in dxs]), *map(held, halves))
+            ordered = (key_rows, value_columns)
         else:
-            result = pl.pallas_call(
-                functools.partial(next_kernel, d),
-                out_shape=piece,
-                in_specs=[smem] + [vmem] * 3,
-                out_specs=vmem,
+            results = pl.pallas_call(
+                functools.partial(next_kernel, dxs),
+                out_shape=(piece,) * n,
+                in_specs=[smem] + [vmem] * (n + 2),
+                out_specs=(vmem,) * n,
                 scratch_shapes=scratch,
                 compiler_params=room(24),
-            )(marked, *map(held, (moved[d], *ordered)))
-        handed[d] = lax.ppermute(result, AXES, route(-d, 1))
+            )(marked, *map(held, [moved[d] for d in dxs]), *map(held, ordered))
+        for d, result in zip(dxs, results):
+            handed[d] = lax.ppermute(result, AXES, route(-d, 1))
     out = None
-    for d in (2, 1, 3, 0):
+    for d in sum(CALLS, ()):
         out = place(handed[d], out, (marked[:1] + d) % 4)
     return out
 

time: 103 us -> 102 us (level)
  Pallas kernels: 21.1 us -> 18.9 us
  starting transfers between devices: 57.4 us -> 58.6 us
    pallas_call x4, Pallas kernels: 15.3 us -> 13.1 us  [the longest x3 8.66 us: layer(): pl.pallas_call(functools.partial(next_kernel, dxs), out_shape=(piece,) *...]
    ppermute x4, starting transfers between devices: 13.6 us -> 14.8 us  [layer(): handed[d] = lax.ppermute(result, AXES, route(-d, 1))]
  transfers between devices with their start and end apart: 14 -> 14, of which waited for: 3 -> 3; matrix products, arithmetic and copies ran while one was open for 0% -> 0% of each run, Pallas kernels for 18% -> 17%
where the time goes in v3:
time: 102 us; the launch traced here: 101 us
  starting transfers between devices  58.6 us (57%)
  Pallas kernels  18.9 us (19%)
  waiting for transfers between devices  11 us (11%)
  blocking collectives  10.2 us (10%)
  between operations  1.9 us (2%)
    ppermute x4, starting transfers between devices, layer(): handed[d] = lax.ppermute(result, AXES, route(-d, 1))  14.8 us
    ppermute x4, waiting for transfers between devices, layer(): handed[d] = lax.ppermute(result, AXES, route(-d, 1))  10.9 us
    all_to_all x1, blocking collectives, layer(): mine = lax.all_to_all(kv, 'x', 0, 0, tiled=True)  10.2 us
    ppermute x3, starting transfers between devices, layer(): moved[d] = lax.ppermute(packed[d], AXES, route(d, 0))  9.08 us
    pallas_call x3, Pallas kernels, layer(): pl.pallas_call(functools.partial(next_kernel, dxs), out_shape=(piece,) *...  8.66 us
    ppermute x1, starting transfers between devices, layer(): twin = swap_cores(mine)  7.3 us
    ppermute x1, starting transfers between devices, layer(): near_mine = pass_on(mine)  5.9 us
    ppermute x1, starting transfers between devices, layer(): far_mine = pass_on(near_mine)  5.75 us
  transfers between devices with their start and end apart: 14, of which 3 were waited for; matrix products, arithmetic and copies ran while one was open for 0% of the time, Pallas kernels for 17%

profile of v3, /device:TPU:1, one launch (start us, length us, event | category | flops | bytes accessed | tf_op | source)
XLA Modules:
  0.0 101.2 jit_solution(11649823065181061977)
XLA Ops:
  2.1 1.4 %pack_keys.1 = bf16[4,128,256]{2,1,0:T(8,128)(2,1)S(1)} custom-call(s32[9]{0:T(128)S(1)} %concatenate.3.scalars, f32[1,128]{1,0:T(1,128)} %constant.62.clone.freq_ref, bf16[128,512]{1,0:T(8,128)(2,1)} %bitcast.15, bf16[128,512]{1,0:T(8,128)(2,1)} %bitcast.16), custom_call_target="tpu_custom_call" | custom-call | tf_op jit(solution)/shard_map/pack_keys/pallas_call | solution.py:249
  3.5 10.2 %all_to_all.5.refs_1_ = bf16[4,128,256]{2,1,0:T(8,128)(2,1)S(1)} all-to-all(bf16[4,128,256]{2,1,0:T(8,128)(2,1)S(1)} %pack_keys.1), channel_id=1, replica_groups=mesh['x'=4,'yh'=4,'c'=2,'yl'=2,'z'=12] {'x'}, dimensions={0} | all-to-all | bytes 524288 | tf_op jit(solution)/shard_map/all_to_all | solution.py:265
  13.6 5.9 %collective-permute-start.2 = (bf16[4,128,256]{2,1,0:T(8,128)(2,1)S(1)}, bf16[4,128,256]{2,1,0:T(8,128)(2,1)S(1)}, u32[]{:S(2)}, u32[]{:S(2)}) collective-permute-start(bf16[4,128,256]{2,1,0:T(8,128)(2,1)S(1)} %all_to_all.5.refs_1_), channel_id=1, source_target_pairs={{0,48},{24,168},{48,96},{72,24},{96,144},{120,72},{144,0},{168,120... | collective-permute-start | bytes 786440 | tf_op jit(solution)/shard_map/ppermute | solution.py:269
  19.6 7.3 %collective-permute-start.1 = (bf16[4,128,256]{2,1,0:T(8,128)(2,1)S(1)}, bf16[4,128,256]{2,1,0:T(8,128)(2,1)S(1)}, u32[]{:S(2)}, u32[]{:S(2)}) collective-permute-start(bf16[4,128,256]{2,1,0:T(8,128)(2,1)S(1)} %all_to_all.5.refs_1_), channel_id=1, source_target_pairs={{0,24},{24,0},{1,25},{25,1},{2,26},{26,2},{3,27},{27,3},{4,28},{28... | collective-permute-start | bytes 786440 | tf_op jit(solution)/shard_map/ppermute | solution.py:270
  26.9 5.8 %collective-permute-start.6 = (bf16[4,128,256]{2,1,0:T(8,128)(2,1)S(1)}, bf16[4,128,256]{2,1,0:T(8,128)(2,1)S(1)}, u32[]{:S(2)}, u32[]{:S(2)}) collective-permute-start(bf16[4,128,256]{2,1,0:T(8,128)(2,1)S(1)} %collective-permute-done.2.refs_3_), channel_id=1, source_target_pairs={{0,48},{24,168},{48,96},{72,24},{96,144},{120,72},{144,0},{168,120... | collective-permute-start | bytes 786440 | tf_op jit(solution)/shard_map/ppermute | solution.py:272
  32.6 1.9 %collective-permute-start.3 = (bf16[4,128,256]{2,1,0:T(8,128)(2,1)S(1)}, bf16[4,128,256]{2,1,0:T(8,128)(2,1)S(1)}, u32[]{:S(2)}, u32[]{:S(2)}) collective-permute-start(bf16[4,128,256]{2,1,0:T(8,128)(2,1)S(1)} %collective-permute-done.1.refs_2_), channel_id=1, source_target_pairs={{0,48},{24,168},{48,96},{72,24},{96,144},{120,72},{144,0},{168,120... | collective-permute-start | bytes 786440 | tf_op jit(solution)/shard_map/ppermute | solution.py:271
  34.6 1.5 %pack_queries.1 = (bf16[128,1024]{1,0:T(8,128)(2,1)S(1)}, bf16[128,1024]{1,0:T(8,128)(2,1)S(1)}, bf16[128,1024]{1,0:T(8,128)(2,1)S(1)}, bf16[128,1024]{1,0:T(8,128)(2,1)S(1)}) custom-call(s32[9]{0:T(128)S(1)} %concatenate.3.scalars, f32[1,128]{1,0:T(1,128)} %constant.62.clone.freq_ref, bf16[128,4096]{1,0:T(8,128)(2,1)S(1)} %bitcast.8), custom_call_target="tpu_custom_call" | custom-call | tf_op jit(solution)/shard_map/pack_queries/pallas_call | solution.py:257
  36.1 2.6 %collective-permute-start = (bf16[128,1024]{1,0:T(8,128)(2,1)S(1)}, bf16[128,1024]{1,0:T(8,128)(2,1)S(1)}, u32[]{:S(2)}, u32[]{:S(2)}) collective-permute-start(bf16[128,1024]{1,0:T(8,128)(2,1)S(1)} %get-tuple-element.13), channel_id=1, source_target_pairs={{0,384},{1,385},{2,386},{3,387},{4,388},{5,389},{6,390},{7,391},{8... | collective-permute-start | bytes 786440 | tf_op jit(solution)/shard_map/ppermute | solution.py:279
  38.7 5.4 %collective-permute-start.5 = (bf16[4,128,256]{2,1,0:T(8,128)(2,1)S(1)}, bf16[4,128,256]{2,1,0:T(8,128)(2,1)S(1)}, u32[]{:S(2)}, u32[]{:S(2)}) collective-permute-start(bf16[4,128,256]{2,1,0:T(8,128)(2,1)S(1)} %collective-permute-done.2.refs_3_), channel_id=1, source_target_pairs={{0,24},{24,0},{1,25},{25,1},{2,26},{26,2},{3,27},{27,3},{4,28},{28... | collective-permute-start | bytes 786440 | tf_op jit(solution)/shard_map/ppermute | solution.py:273
  44.1 5.7 %collective-permute-start.7 = (bf16[4,128,256]{2,1,0:T(8,128)(2,1)S(1)}, bf16[4,128,256]{2,1,0:T(8,128)(2,1)S(1)}, u32[]{:S(2)}, u32[]{:S(2)}) collective-permute-start(bf16[4,128,256]{2,1,0:T(8,128)(2,1)S(1)} %collective-permute-done.6.refs_7_), channel_id=1, source_target_pairs={{0,24},{24,0},{1,25},{25,1},{2,26},{26,2},{3,27},{27,3},{4,28},{28... | collective-permute-start | bytes 786440 | tf_op jit(solution)/shard_map/ppermute | solution.py:275
  49.9 2.8 %collective-permute-start.4 = (bf16[4,128,256]{2,1,0:T(8,128)(2,1)S(1)}, bf16[4,128,256]{2,1,0:T(8,128)(2,1)S(1)}, u32[]{:S(2)}, u32[]{:S(2)}) collective-permute-start(bf16[4,128,256]{2,1,0:T(8,128)(2,1)S(1)} %collective-permute-done.3.refs_4_), channel_id=1, source_target_pairs={{0,24},{24,0},{1,25},{25,1},{2,26},{26,2},{3,27},{27,3},{4,28},{28... | collective-permute-start | bytes 786440 | tf_op jit(solution)/shard_map/ppermute | solution.py:274
  52.7 2.2 %collective-permute-start.11 = (bf16[128,1024]{1,0:T(8,128)(2,1)S(1)}, bf16[128,1024]{1,0:T(8,128)(2,1)S(1)}, u32[]{:S(2)}, u32[]{:S(2)}) collective-permute-start(bf16[128,1024]{1,0:T(8,128)(2,1)S(1)} %get-tuple-element.17), channel_id=1, source_target_pairs={{0,192},{1,193},{2,194},{3,195},{4,196},{5,197},{6,198},{7,199},{8... | collective-permute-start | bytes 786440 | tf_op jit(solution)/shard_map/ppermute | solution.py:279
  54.9 4.3 %collective-permute-start.9 = (bf16[128,1024]{1,0:T(8,128)(2,1)S(1)}, bf16[128,1024]{1,0:T(8,128)(2,1)S(1)}, u32[]{:S(2)}, u32[]{:S(2)}) collective-permute-start(bf16[128,1024]{1,0:T(8,128)(2,1)S(1)} %get-tuple-element.16), channel_id=1, source_target_pairs={{0,576},{1,577},{2,578},{3,579},{4,580},{5,581},{6,582},{7,583},{8... | collective-permute-start | bytes 786440 | tf_op jit(solution)/shard_map/ppermute | solution.py:279
  59.2 4.4 %shard_map.73 = (bf16[128,1024]{1,0:T(8,128)(2,1)S(1)}, bf16[4608,128]{1,0:T(8,128)(2,1)S(1)}, bf16[144,4608]{1,0:T(8,128)(2,1)S(1)}) custom-call(s32[9]{0:T(128)S(1)} %broadcast_minimum_fusion.scalars, bf16[128,1024]{1,0:T(8,128)(2,1)S(1)} %collective-permute-done.refs_0_, bf16[4,128,256]{2,1,0:T(8,128)(2,1)S(1)} %all_to_all.5.refs_1_, ...), custom_call_target="tpu_custom_call" | custom-call | tf_op jit(solution)/shard_map/pallas_call | solution.py:295
  63.7 3.7 %shard_map.76 = bf16[128,1024]{1,0:T(8,128)(2,1)S(1)} custom-call(s32[9]{0:T(128)S(1)} %broadcast_minimum_fusion.scalars, bf16[128,1024]{1,0:T(8,128)(2,1)S(1)} %collective-permute-done.11.refs_0_, bf16[4608,128]{1,0:T(8,128)(2,1)S(1)} %get-tuple-element.14.refs_1_, bf16[144,4608]{1,0:T(8,128)(2,1)S(1)} %get-tuple-element.15.refs_2_), custom_call_target="tpu_custom_call" | custom-call | tf_op jit(solution)/shard_map/pallas_call | solution.py:305
  67.4 1.9 %collective-permute-start.12 = (bf16[128,1024]{1,0:T(8,128)(2,1)S(1)}, bf16[128,1024]{1,0:T(8,128)(2,1)S(1)}, u32[]{:S(2)}, u32[]{:S(2)}) collective-permute-start(bf16[128,1024]{1,0:T(8,128)(2,1)S(1)} %shard_map.76), channel_id=1, source_target_pairs={{0,577},{1,578},{2,579},{3,580},{4,581},{5,582},{6,583},{7,584},{8... | collective-permute-start | bytes 786440 | tf_op jit(solution)/shard_map/ppermute | solution.py:314
  69.3 3.6 %collective-permute-start.13 = (bf16[128,1024]{1,0:T(8,128)(2,1)S(1)}, bf16[128,1024]{1,0:T(8,128)(2,1)S(1)}, u32[]{:S(2)}, u32[]{:S(2)}) collective-permute-start(bf16[128,1024]{1,0:T(8,128)(2,1)S(1)} %get-tuple-element.18), channel_id=1, source_target_pairs={{0,385},{1,386},{2,387},{3,388},{4,389},{5,390},{6,391},{7,392},{8... | collective-permute-start | bytes 786440 | tf_op jit(solution)/shard_map/ppermute | solution.py:314
  73.0 2.5 %shard_map.75 = bf16[128,1024]{1,0:T(8,128)(2,1)S(1)} custom-call(s32[9]{0:T(128)S(1)} %broadcast_minimum_fusion.scalars, bf16[128,1024]{1,0:T(8,128)(2,1)S(1)} %collective-permute-done.9.refs_0_, bf16[4608,128]{1,0:T(8,128)(2,1)S(1)} %get-tuple-element.14.refs_1_, bf16[144,4608]{1,0:T(8,128)(2,1)S(1)} %get-tuple-element.15.refs_2_), custom_call_target="tpu_custom_call" | custom-call | tf_op jit(solution)/shard_map/pallas_call | solution.py:305
  75.5 4.9 %collective-permute-start.10 = (bf16[128,1024]{1,0:T(8,128)(2,1)S(1)}, bf16[128,1024]{1,0:T(8,128)(2,1)S(1)}, u32[]{:S(2)}, u32[]{:S(2)}) collective-permute-start(bf16[128,1024]{1,0:T(8,128)(2,1)S(1)} %shard_map.75), channel_id=1, source_target_pairs={{0,193},{1,194},{2,195},{3,196},{4,197},{5,198},{6,199},{7,200},{8... | collective-permute-start | bytes 786440 | tf_op jit(solution)/shard_map/ppermute | solution.py:314
  80.4 2.5 %shard_map.74 = bf16[128,1024]{1,0:T(8,128)(2,1)S(1)} custom-call(s32[9]{0:T(128)S(1)} %broadcast_minimum_fusion.scalars, bf16[128,1024]{1,0:T(8,128)(2,1)S(1)} %get-tuple-element.12.refs_0_, bf16[4608,128]{1,0:T(8,128)(2,1)S(1)} %get-tuple-element.14.refs_1_, bf16[144,4608]{1,0:T(8,128)(2,1)S(1)} %get-tuple-element.15.refs_2_), custom_call_target="tpu_custom_call" | custom-call | tf_op jit(solution)/shard_map/pallas_call | solution.py:305
  82.9 4.3 %collective-permute-start.8 = (bf16[128,1024]{1,0:T(8,128)(2,1)S(1)}, bf16[128,1024]{1,0:T(8,128)(2,1)S(1)}, u32[]{:S(2)}, u32[]{:S(2)}) collective-permute-start(bf16[128,1024]{1,0:T(8,128)(2,1)S(1)} %shard_map.74), channel_id=1, source_target_pairs={{0,1},{1,2},{2,3},{3,4},{4,5},{5,6},{6,7},{7,8},{8,9},{9,10},{10,1... | collective-permute-start | bytes 786440 | tf_op jit(solution)/shard_map/ppermute | solution.py:314
  87.4 1.1 %collective-permute-done.13.piece_ref = bf16[128,1024]{1,0:T(8,128)(2,1)S(1)} collective-permute-done((bf16[128,1024]{1,0:T(8,128)(2,1)S(1)}, bf16[128,1024]{1,0:T(8,128)(2,1)S(1)}, u32[]{:S(2)}, u32[]{:S(2)}) %collective-permute-start.13) | collective-permute-done | bytes 262176 | tf_op jit(solution)/shard_map/ppermute | solution.py:314
  90.0 4.9 %collective-permute-done.10.piece_ref = bf16[128,1024]{1,0:T(8,128)(2,1)S(1)} collective-permute-done((bf16[128,1024]{1,0:T(8,128)(2,1)S(1)}, bf16[128,1024]{1,0:T(8,128)(2,1)S(1)}, u32[]{:S(2)}, u32[]{:S(2)}) %collective-permute-start.10) | collective-permute-done | bytes 262176 | tf_op jit(solution)/shard_map/ppermute | solution.py:314
  95.6 5.0 %collective-permute-done.8.piece_ref = bf16[128,1024]{1,0:T(8,128)(2,1)S(1)} collective-permute-done((bf16[128,1024]{1,0:T(8,128)(2,1)S(1)}, bf16[128,1024]{1,0:T(8,128)(2,1)S(1)}, u32[]{:S(2)}, u32[]{:S(2)}) %collective-permute-start.8) | collective-permute-done | bytes 262176 | tf_op jit(solution)/shard_map/ppermute | solution.py:314
  (19 shorter events, 3.6 us)
Async XLA Ops:
  0.0 34.6 %copy-start = (bf16[1,128,4096]{2,1,0:T(8,128)(2,1)S(1)}, bf16[1,128,4096]{2,1,0:T(8,128)(2,1)}, u32[]{:S(2)}) copy-start(bf16[1,128,4096]{2,1,0:T(8,128)(2,1)} %param.7) | copy-start | bytes 3145732
  13.6 13.2 %collective-permute-start.2 = (bf16[4,128,256]{2,1,0:T(8,128)(2,1)S(1)}, bf16[4,128,256]{2,1,0:T(8,128)(2,1)S(1)}, u32[]{:S(2)}, u32[]{:S(2)}) collective-permute-start(bf16[4,128,256]{2,1,0:T(8,128)(2,1)S(1)} %all_to_all.5.refs_1_), channel_id=1, source_target_pairs={{0,48},{24,168},{48,96},{72,24},{96,144},{120,72},{144,0},{168,120... | collective-permute-start | bytes 786440 | tf_op jit(solution)/shard_map/ppermute | solution.py:269
  19.6 13.1 %collective-permute-start.1 = (bf16[4,128,256]{2,1,0:T(8,128)(2,1)S(1)}, bf16[4,128,256]{2,1,0:T(8,128)(2,1)S(1)}, u32[]{:S(2)}, u32[]{:S(2)}) collective-permute-start(bf16[4,128,256]{2,1,0:T(8,128)(2,1)S(1)} %all_to_all.5.refs_1_), channel_id=1, source_target_pairs={{0,24},{24,0},{1,25},{25,1},{2,26},{26,2},{3,27},{27,3},{4,28},{28... | collective-permute-start | bytes 786440 | tf_op jit(solution)/shard_map/ppermute | solution.py:270
  26.9 17.3 %collective-permute-start.6 = (bf16[4,128,256]{2,1,0:T(8,128)(2,1)S(1)}, bf16[4,128,256]{2,1,0:T(8,128)(2,1)S(1)}, u32[]{:S(2)}, u32[]{:S(2)}) collective-permute-start(bf16[4,128,256]{2,1,0:T(8,128)(2,1)S(1)} %collective-permute-done.2.refs_3_), channel_id=1, source_target_pairs={{0,48},{24,168},{48,96},{72,24},{96,144},{120,72},{144,0},{168,120... | collective-permute-start | bytes 786440 | tf_op jit(solution)/shard_map/ppermute | solution.py:272
  32.6 17.2 %collective-permute-start.3 = (bf16[4,128,256]{2,1,0:T(8,128)(2,1)S(1)}, bf16[4,128,256]{2,1,0:T(8,128)(2,1)S(1)}, u32[]{:S(2)}, u32[]{:S(2)}) collective-permute-start(bf16[4,128,256]{2,1,0:T(8,128)(2,1)S(1)} %collective-permute-done.1.refs_2_), channel_id=1, source_target_pairs={{0,48},{24,168},{48,96},{72,24},{96,144},{120,72},{144,0},{168,120... | collective-permute-start | bytes 786440 | tf_op jit(solution)/shard_map/ppermute | solution.py:271
  36.1 18.7 %collective-permute-start = (bf16[128,1024]{1,0:T(8,128)(2,1)S(1)}, bf16[128,1024]{1,0:T(8,128)(2,1)S(1)}, u32[]{:S(2)}, u32[]{:S(2)}) collective-permute-start(bf16[128,1024]{1,0:T(8,128)(2,1)S(1)} %get-tuple-element.13), channel_id=1, source_target_pairs={{0,384},{1,385},{2,386},{3,387},{4,388},{5,389},{6,390},{7,391},{8... | collective-permute-start | bytes 786440 | tf_op jit(solution)/shard_map/ppermute | solution.py:279
  38.7 20.5 %collective-permute-start.5 = (bf16[4,128,256]{2,1,0:T(8,128)(2,1)S(1)}, bf16[4,128,256]{2,1,0:T(8,128)(2,1)S(1)}, u32[]{:S(2)}, u32[]{:S(2)}) collective-permute-start(bf16[4,128,256]{2,1,0:T(8,128)(2,1)S(1)} %collective-permute-done.2.refs_3_), channel_id=1, source_target_pairs={{0,24},{24,0},{1,25},{25,1},{2,26},{26,2},{3,27},{27,3},{4,28},{28... | collective-permute-start | bytes 786440 | tf_op jit(solution)/shard_map/ppermute | solution.py:273
  44.1 15.1 %collective-permute-start.7 = (bf16[4,128,256]{2,1,0:T(8,128)(2,1)S(1)}, bf16[4,128,256]{2,1,0:T(8,128)(2,1)S(1)}, u32[]{:S(2)}, u32[]{:S(2)}) collective-permute-start(bf16[4,128,256]{2,1,0:T(8,128)(2,1)S(1)} %collective-permute-done.6.refs_7_), channel_id=1, source_target_pairs={{0,24},{24,0},{1,25},{25,1},{2,26},{26,2},{3,27},{27,3},{4,28},{28... | collective-permute-start | bytes 786440 | tf_op jit(solution)/shard_map/ppermute | solution.py:275
  49.9 9.4 %collective-permute-start.4 = (bf16[4,128,256]{2,1,0:T(8,128)(2,1)S(1)}, bf16[4,128,256]{2,1,0:T(8,128)(2,1)S(1)}, u32[]{:S(2)}, u32[]{:S(2)}) collective-permute-start(bf16[4,128,256]{2,1,0:T(8,128)(2,1)S(1)} %collective-permute-done.3.refs_4_), channel_id=1, source_target_pairs={{0,24},{24,0},{1,25},{25,1},{2,26},{26,2},{3,27},{27,3},{4,28},{28... | collective-permute-start | bytes 786440 | tf_op jit(solution)/shard_map/ppermute | solution.py:274
  52.7 11.0 %collective-permute-start.11 = (bf16[128,1024]{1,0:T(8,128)(2,1)S(1)}, bf16[128,1024]{1,0:T(8,128)(2,1)S(1)}, u32[]{:S(2)}, u32[]{:S(2)}) collective-permute-start(bf16[128,1024]{1,0:T(8,128)(2,1)S(1)} %get-tuple-element.17), channel_id=1, source_target_pairs={{0,192},{1,193},{2,194},{3,195},{4,196},{5,197},{6,198},{7,199},{8... | collective-permute-start | bytes 786440 | tf_op jit(solution)/shard_map/ppermute | solution.py:279
  54.9 18.1 %collective-permute-start.9 = (bf16[128,1024]{1,0:T(8,128)(2,1)S(1)}, bf16[128,1024]{1,0:T(8,128)(2,1)S(1)}, u32[]{:S(2)}, u32[]{:S(2)}) collective-permute-start(bf16[128,1024]{1,0:T(8,128)(2,1)S(1)} %get-tuple-element.16), channel_id=1, source_target_pairs={{0,576},{1,577},{2,578},{3,579},{4,580},{5,581},{6,582},{7,583},{8... | collective-permute-start | bytes 786440 | tf_op jit(solution)/shard_map/ppermute | solution.py:279
  67.4 21.9 %collective-permute-start.12 = (bf16[128,1024]{1,0:T(8,128)(2,1)S(1)}, bf16[128,1024]{1,0:T(8,128)(2,1)S(1)}, u32[]{:S(2)}, u32[]{:S(2)}) collective-permute-start(bf16[128,1024]{1,0:T(8,128)(2,1)S(1)} %shard_map.76), channel_id=1, source_target_pairs={{0,577},{1,578},{2,579},{3,580},{4,581},{5,582},{6,583},{7,584},{8... | collective-permute-start | bytes 786440 | tf_op jit(solution)/shard_map/ppermute | solution.py:314
  69.3 19.2 %collective-permute-start.13 = (bf16[128,1024]{1,0:T(8,128)(2,1)S(1)}, bf16[128,1024]{1,0:T(8,128)(2,1)S(1)}, u32[]{:S(2)}, u32[]{:S(2)}) collective-permute-start(bf16[128,1024]{1,0:T(8,128)(2,1)S(1)} %get-tuple-element.18), channel_id=1, source_target_pairs={{0,385},{1,386},{2,387},{3,388},{4,389},{5,390},{6,391},{7,392},{8... | collective-permute-start | bytes 786440 | tf_op jit(solution)/shard_map/ppermute | solution.py:314
  75.5 19.4 %collective-permute-start.10 = (bf16[128,1024]{1,0:T(8,128)(2,1)S(1)}, bf16[128,1024]{1,0:T(8,128)(2,1)S(1)}, u32[]{:S(2)}, u32[]{:S(2)}) collective-permute-start(bf16[128,1024]{1,0:T(8,128)(2,1)S(1)} %shard_map.75), channel_id=1, source_target_pairs={{0,193},{1,194},{2,195},{3,196},{4,197},{5,198},{6,199},{7,200},{8... | collective-permute-start | bytes 786440 | tf_op jit(solution)/shard_map/ppermute | solution.py:314
  82.9 17.7 %collective-permute-start.8 = (bf16[128,1024]{1,0:T(8,128)(2,1)S(1)}, bf16[128,1024]{1,0:T(8,128)(2,1)S(1)}, u32[]{:S(2)}, u32[]{:S(2)}) collective-permute-start(bf16[128,1024]{1,0:T(8,128)(2,1)S(1)} %shard_map.74), channel_id=1, source_target_pairs={{0,1},{1,2},{2,3},{3,4},{4,5},{5,6},{6,7},{7,8},{8,9},{9,10},{10,1... | collective-permute-start | bytes 786440 | tf_op jit(solution)/shard_map/ppermute | solution.py:314

commit v4 on v3

--- a/solution.py
+++ b/solution.py
@@ -57,38 +57,44 @@
 LENGTHS, NUMERATOR, DENOMINATOR = 3, 7, 8
 
 
-def doc_start(position, scalars):
+def lengths_of(scalars):
+    return [scalars[LENGTHS + d] for d in range(4)]
+
+
+def doc_start(position, lengths):
     end = 0
     start = jnp.zeros_like(position)
-    for d in range(4):
-        length = scalars[LENGTHS + d]
+    for length in lengths:
         end = end + length
         start = start + jnp.where(position >= end, length, 0)
     return start
 
 
-def rotation(scalars, freq_ref, scale):
-    shard = scalars[0] * 8 + scalars[1] * 2 + scalars[2]
+def rotation(shard, lengths, ratio, freq_ref, scale):
     row = lax.broadcasted_iota(jnp.int32, (128, HEAD), 0)
     lane = lax.broadcasted_iota(jnp.int32, (128, HEAD), 1)
     position = jnp.where(row < SPAN, shard * SPAN + row, (63 - shard) * SPAN + row - SPAN)
-    offset = (position - doc_start(position, scalars)).astype(jnp.float32)
-    ratio = jnp.full((128, HEAD), scalars[NUMERATOR], jnp.int32).astype(jnp.float32) / jnp.full(
-        (128, HEAD), scalars[DENOMINATOR], jnp.int32
-    ).astype(jnp.float32)
+    offset = (position - doc_start(position, lengths)).astype(jnp.float32)
     angle = offset * ratio * freq_ref[...]
     cosine = jnp.cos(angle) * scale
     sine = jnp.sin(angle) * scale
     return cosine, jnp.where(lane < HEAD // 2, -sine, sine)
 
 
+def ratio_of(numerator, denominator):
+    top = jnp.full((128, HEAD), numerator, jnp.int32).astype(jnp.float32)
+    return top / jnp.full((128, HEAD), denominator, jnp.int32).astype(jnp.float32)
+
+
 def turn(part, cosine, sine):
     wide = part.astype(jnp.float32)
     return (wide * cosine + pltpu.roll(wide, HEAD // 2, 1) * sine).astype(jnp.bfloat16)
 
 
-def pack_keys_kernel(scalars, freq_ref, k_ref, v_ref, kv_ref):
-    cosine, sine = rotation(scalars, freq_ref, 1.0)
+def pack_keys_kernel(lengths_ref, num_ref, den_ref, freq_ref, k_ref, v_ref, kv_ref):
+    shard = lax.axis_index("x") * 8 + lax.axis_index("yh") * 2 + lax.axis_index("c")
+    lengths = [lengths_ref[0, d] for d in range(4)]
+    cosine, sine = rotation(shard, lengths, ratio_of(num_ref[0], den_ref[0]), freq_ref, 1.0)
     for h in range(KV_HEADS):
         cols = slice(h * HEAD, (h + 1) * HEAD)
         kv_ref[h, :, :HEAD] = turn(k_ref[:, cols], cosine, sine)
@@ -96,7 +102,9 @@
 
 
 def pack_queries_kernel(scalars, freq_ref, q_ref, *q_out):
-    cosine, sine = rotation(scalars, freq_ref, QUERY_SCALE)
+    shard = scalars[0] * 8 + scalars[1] * 2 + scalars[2]
+    ratio = ratio_of(scalars[NUMERATOR], scalars[DENOMINATOR])
+    cosine, sine = rotation(shard, lengths_of(scalars), ratio, freq_ref, QUERY_SCALE)
     for d in range(4):
         group = lax.rem(scalars[0] + d, 4)
         for h in range(GROUP):
@@ -104,16 +112,19 @@
             q_out[d][:, h * HEAD : (h + 1) * HEAD] = turn(q_ref[:, pl.ds(start, HEAD)], cosine, sine)
 
 
-def gather_keys(scalars, blocks, k_ref, vt_ref):
+def gather_keys(scalars, halves, far_ref, k_ref, vt_ref):
     yh, core = scalars[1], scalars[2]
     sides = (0, 2 * core - 1, 1 - 2 * core, 2)
-    for (mine, others), side in zip(blocks, sides):
+    for g, side in enumerate(sides):
         y = lax.rem(yh + side + 4, 4)
         for x in range(4):
             early = pl.multiple_of((x * 8 + y * 2) * SPAN, 2 * SPAN)
             late = pl.multiple_of((62 - x * 8 - y * 2) * SPAN, 2 * SPAN)
-            m, o = mine[x], others[x]
-            zero, one = jnp.where(core == 0, m, o), jnp.where(core == 0, o, m)
+            if g == 3:
+                zero, one = far_ref[0, x], far_ref[1, x]
+            else:
+                m, o = halves[2 * g][x], halves[2 * g + 1][x]
+                zero, one = jnp.where(core == 0, m, o), jnp.where(core == 0, o, m)
             k_ref[pl.ds(early, 2 * SPAN), :] = jnp.concatenate(
                 [zero[:SPAN, :HEAD], one[:SPAN, :HEAD]], axis=0
             )
@@ -138,13 +149,13 @@
         rows = pl.ds(pl.multiple_of(half * SPAN, SPAN), SPAN)
         block = jnp.where(half == 0, shard, 63 - shard)
         first = block * SPAN
-        low = lax.div(doc_start(first, scalars), HEAD) * HEAD
+        low = lax.div(doc_start(first, lengths_of(scalars)), HEAD) * HEAD
         count = lax.div(first - low, TILE) + 1
         q_tile = jnp.concatenate(
             [q_ref[rows, h * HEAD : (h + 1) * HEAD] for h in range(GROUP)], axis=0
         )
         q_pos = first + token
-        q_start = doc_start(q_pos, scalars)
+        q_start = doc_start(q_pos, lengths_of(scalars))
         m_scr[...] = jnp.full(m_scr.shape, MASKED, jnp.float32)
         acc_scr[...] = jnp.zeros_like(acc_scr)
 
@@ -199,10 +210,11 @@
 
 def first_kernel(dxs, scalars, *refs):
     n = len(dxs)
-    queries, halves, outs, (k_ref, vt_ref) = refs[:n], refs[n : n + 8], refs[n + 8 : 2 * n + 8], refs[2 * n + 8 : 2 * n + 10]
-    gather_keys(scalars, [halves[i : i + 2] for i in range(0, 8, 2)], k_ref, vt_ref)
+    queries, halves, far_ref = refs[:n], refs[n : n + 6], refs[n + 6]
+    outs, (k_ref, vt_ref) = refs[n + 7 : 2 * n + 7], refs[2 * n + 7 : 2 * n + 9]
+    gather_keys(scalars, halves, far_ref, k_ref, vt_ref)
     for dx, q_ref, o_ref in zip(dxs, queries, outs):
-        attend_block(scalars, dx, q_ref, k_ref, vt_ref, o_ref, *refs[2 * n + 10 :])
+        attend_block(scalars, dx, q_ref, k_ref, vt_ref, o_ref, *refs[2 * n + 9 :])
 
 
 def next_kernel(dxs, scalars, *refs):
@@ -249,11 +261,11 @@
     kv = pl.pallas_call(
         pack_keys_kernel,
         out_shape=pltpu.VMEM((4, 128, 2 * HEAD), bf16),
-        in_specs=[smem] + [vmem] * 3,
+        in_specs=[smem] * 3 + [vmem] * 3,
         out_specs=vmem,
         name="pack_keys",
         compiler_params=room(12),
-    )(scalars, freq, in_hbm(keys[0]), in_hbm(values[0]))
+    )(in_hbm(doc_lengths), interp_num, interp_den, freq, in_hbm(keys[0]), in_hbm(values[0]))
     packed = pl.pallas_call(
         pack_queries_kernel,
         out_shape=(piece,) * 4,
@@ -272,8 +284,8 @@
     far_mine = pass_on(near_mine)
     other_a = swap_cores(near_mine)
     other_b = swap_cores(near_twin)
-    far_twin = swap_cores(far_mine)
-    halves = (mine, twin, near_mine, near_twin, other_b, other_a, far_mine, far_twin)
+    far = lax.all_gather(far_mine, "c", axis=0)
+    blocks = (mine, twin, near_mine, near_twin, other_b, other_a, far)
     moved = {0: packed[0]}
     for d in (2, 1, 3):
         moved[d] = lax.ppermute(packed[d], AXES, route(d, 0))
@@ -295,11 +307,11 @@
             *results, key_rows, value_columns = pl.pallas_call(
                 functools.partial(first_kernel, dxs),
                 out_shape=(piece,) * n + laid_out,
-                in_specs=[smem] + [vmem] * (n + 8),
+                in_specs=[smem] + [vmem] * (n + 7),
                 out_specs=(vmem,) * (n + 2),
                 scratch_shapes=scratch,
                 compiler_params=room(24),
-            )(marked, *map(held, [moved[d] for d in dxs]), *map(held, halves))
+            )(marked, *map(held, [moved[d] for d in dxs]), *map(held, blocks))
             ordered = (key_rows, value_columns)
         else:
             results = pl.pallas_call(

time: 102 us -> 102 us (level)
  starting transfers between devices: 58.6 us -> 56.2 us
  blocking collectives: 10.2 us -> 12.5 us
    ppermute x1 -> x0, starting transfers between devices: 5.7 us -> none  [layer(): far_twin = swap_cores(far_mine)]
    ppermute x4, starting transfers between devices: 14.8 us -> 18.4 us  [layer(): handed[d] = lax.ppermute(result, AXES, route(-d, 1))]
    all_gather x0 -> x1, blocking collectives: none -> 2.31 us  [layer(): far = lax.all_gather(far_mine, 'c', axis=0)]
  transfers between devices with their start and end apart: 14 -> 13, of which waited for: 3 -> 3; matrix products, arithmetic and copies ran while one was open for 0% -> 1% of each run, Pallas kernels for 17% -> 17%
where the time goes in v4:
time: 102 us; the launch traced here: 101 us
  starting transfers between devices  56.2 us (55%)
  Pallas kernels  18.9 us (19%)
  blocking collectives  12.5 us (12%)
  waiting for transfers between devices  11.4 us (11%)
  between operations  1.87 us (2%)
    ppermute x4, starting transfers between devices, layer(): handed[d] = lax.ppermute(result, AXES, route(-d, 1))  18.4 us
    ppermute x4, waiting for transfers between devices, layer(): handed[d] = lax.ppermute(result, AXES, route(-d, 1))  11.3 us
    all_to_all x1, blocking collectives, layer(): mine = lax.all_to_all(kv, 'x', 0, 0, tiled=True)  10.2 us
    ppermute x3, starting transfers between devices, layer(): moved[d] = lax.ppermute(packed[d], AXES, route(d, 0))  9.08 us
    pallas_call x3, Pallas kernels, layer(): pl.pallas_call(functools.partial(next_kernel, dxs), out_shape=(piece,) *...  8.66 us
    ppermute x1, starting transfers between devices, layer(): twin = swap_cores(mine)  7.3 us
    ppermute x1, starting transfers between devices, layer(): other_a = swap_cores(near_mine)  5.96 us
    ppermute x1, starting transfers between devices, layer(): near_mine = pass_on(mine)  5.9 us
  transfers between devices with their start and end apart: 13, of which 3 were waited for; matrix products, arithmetic and copies ran while one was open for 1% of the time, Pallas kernels for 17%

profile of v4, /device:TPU:1, one launch (start us, length us, event | category | flops | bytes accessed | tf_op | source)
XLA Modules:
  0.0 101.5 jit_solution(7118713990240609286)
XLA Ops:
  1.4 1.4 %pack_keys.1 = bf16[4,128,256]{2,1,0:T(8,128)(2,1)S(1)} custom-call(s32[1,4]{1,0:T(1,128)} %lengths_ref.1, s32[1]{0:T(128)S(6)} %copy.14.num_ref, s32[1]{0:T(128)S(6)} %copy.15.den_ref, f32[1,128]{1,0:T(1,128)} %constant.62.clone.freq_ref, bf16[128,512]{1,0:T(8,128)(2,1)} %bitcast.17, bf16[128,512]{1,0:T(8,128)(2,1)} %bitcast.18), custom_call_target="tpu_custom_call" | custom-call | tf_op jit(solution)/shard_map/pack_keys/pallas_call | solution.py:261
  2.8 10.2 %all_to_all.5.refs_1_ = bf16[4,128,256]{2,1,0:T(8,128)(2,1)S(1)} all-to-all(bf16[4,128,256]{2,1,0:T(8,128)(2,1)S(1)} %pack_keys.1), channel_id=1, replica_groups=mesh['x'=4,'yh'=4,'c'=2,'yl'=2,'z'=12] {'x'}, dimensions={0} | all-to-all | bytes 524288 | tf_op jit(solution)/shard_map/all_to_all | solution.py:277
  12.9 5.9 %collective-permute-start.2 = (bf16[4,128,256]{2,1,0:T(8,128)(2,1)S(1)}, bf16[4,128,256]{2,1,0:T(8,128)(2,1)S(1)}, u32[]{:S(2)}, u32[]{:S(2)}) collective-permute-start(bf16[4,128,256]{2,1,0:T(8,128)(2,1)S(1)} %all_to_all.5.refs_1_), channel_id=1, source_target_pairs={{0,48},{24,168},{48,96},{72,24},{96,144},{120,72},{144,0},{168,120... | collective-permute-start | bytes 786440 | tf_op jit(solution)/shard_map/ppermute | solution.py:281
  18.8 7.3 %collective-permute-start.1 = (bf16[4,128,256]{2,1,0:T(8,128)(2,1)S(1)}, bf16[4,128,256]{2,1,0:T(8,128)(2,1)S(1)}, u32[]{:S(2)}, u32[]{:S(2)}) collective-permute-start(bf16[4,128,256]{2,1,0:T(8,128)(2,1)S(1)} %all_to_all.5.refs_1_), channel_id=1, source_target_pairs={{0,24},{24,0},{1,25},{25,1},{2,26},{26,2},{3,27},{27,3},{4,28},{28... | collective-permute-start | bytes 786440 | tf_op jit(solution)/shard_map/ppermute | solution.py:282
  26.1 5.8 %collective-permute-start.6 = (bf16[4,128,256]{2,1,0:T(8,128)(2,1)S(1)}, bf16[4,128,256]{2,1,0:T(8,128)(2,1)S(1)}, u32[]{:S(2)}, u32[]{:S(2)}) collective-permute-start(bf16[4,128,256]{2,1,0:T(8,128)(2,1)S(1)} %collective-permute-done.2.refs_3_), channel_id=1, source_target_pairs={{0,48},{24,168},{48,96},{72,24},{96,144},{120,72},{144,0},{168,120... | collective-permute-start | bytes 786440 | tf_op jit(solution)/shard_map/ppermute | solution.py:284
  31.9 1.9 %collective-permute-start.3 = (bf16[4,128,256]{2,1,0:T(8,128)(2,1)S(1)}, bf16[4,128,256]{2,1,0:T(8,128)(2,1)S(1)}, u32[]{:S(2)}, u32[]{:S(2)}) collective-permute-start(bf16[4,128,256]{2,1,0:T(8,128)(2,1)S(1)} %collective-permute-done.1.refs_2_), channel_id=1, source_target_pairs={{0,48},{24,168},{48,96},{72,24},{96,144},{120,72},{144,0},{168,120... | collective-permute-start | bytes 786440 | tf_op jit(solution)/shard_map/ppermute | solution.py:283
  33.8 0.7 concatenate.3.scalars
  34.6 1.5 %pack_queries.1 = (bf16[128,1024]{1,0:T(8,128)(2,1)S(1)}, bf16[128,1024]{1,0:T(8,128)(2,1)S(1)}, bf16[128,1024]{1,0:T(8,128)(2,1)S(1)}, bf16[128,1024]{1,0:T(8,128)(2,1)S(1)}) custom-call(s32[9]{0:T(128)S(1)} %concatenate.3.scalars, f32[1,128]{1,0:T(1,128)} %constant.62.clone.freq_ref, bf16[128,4096]{1,0:T(8,128)(2,1)S(1)} %bitcast.10), custom_call_target="tpu_custom_call" | custom-call | tf_op jit(solution)/shard_map/pack_queries/pallas_call | solution.py:269
  36.1 2.6 %collective-permute-start = (bf16[128,1024]{1,0:T(8,128)(2,1)S(1)}, bf16[128,1024]{1,0:T(8,128)(2,1)S(1)}, u32[]{:S(2)}, u32[]{:S(2)}) collective-permute-start(bf16[128,1024]{1,0:T(8,128)(2,1)S(1)} %get-tuple-element.13), channel_id=1, source_target_pairs={{0,384},{1,385},{2,386},{3,387},{4,388},{5,389},{6,390},{7,391},{8... | collective-permute-start | bytes 786440 | tf_op jit(solution)/shard_map/ppermute | solution.py:291
  38.7 2.7 %collective-permute-start.10 = (bf16[128,1024]{1,0:T(8,128)(2,1)S(1)}, bf16[128,1024]{1,0:T(8,128)(2,1)S(1)}, u32[]{:S(2)}, u32[]{:S(2)}) collective-permute-start(bf16[128,1024]{1,0:T(8,128)(2,1)S(1)} %get-tuple-element.17), channel_id=1, source_target_pairs={{0,192},{1,193},{2,194},{3,195},{4,196},{5,197},{6,198},{7,199},{8... | collective-permute-start | bytes 786440 | tf_op jit(solution)/shard_map/ppermute | solution.py:291
  41.4 3.8 %collective-permute-start.8 = (bf16[128,1024]{1,0:T(8,128)(2,1)S(1)}, bf16[128,1024]{1,0:T(8,128)(2,1)S(1)}, u32[]{:S(2)}, u32[]{:S(2)}) collective-permute-start(bf16[128,1024]{1,0:T(8,128)(2,1)S(1)} %get-tuple-element.16), channel_id=1, source_target_pairs={{0,576},{1,577},{2,578},{3,579},{4,580},{5,581},{6,582},{7,583},{8... | collective-permute-start | bytes 786440 | tf_op jit(solution)/shard_map/ppermute | solution.py:291
  45.2 6.0 %collective-permute-start.5 = (bf16[4,128,256]{2,1,0:T(8,128)(2,1)S(1)}, bf16[4,128,256]{2,1,0:T(8,128)(2,1)S(1)}, u32[]{:S(2)}, u32[]{:S(2)}) collective-permute-start(bf16[4,128,256]{2,1,0:T(8,128)(2,1)S(1)} %collective-permute-done.2.refs_3_), channel_id=1, source_target_pairs={{0,24},{24,0},{1,25},{25,1},{2,26},{26,2},{3,27},{27,3},{4,28},{28... | collective-permute-start | bytes 786440 | tf_op jit(solution)/shard_map/ppermute | solution.py:285
  51.2 1.9 %collective-permute-start.4 = (bf16[4,128,256]{2,1,0:T(8,128)(2,1)S(1)}, bf16[4,128,256]{2,1,0:T(8,128)(2,1)S(1)}, u32[]{:S(2)}, u32[]{:S(2)}) collective-permute-start(bf16[4,128,256]{2,1,0:T(8,128)(2,1)S(1)} %collective-permute-done.3.refs_4_), channel_id=1, source_target_pairs={{0,24},{24,0},{1,25},{25,1},{2,26},{26,2},{3,27},{27,3},{4,28},{28... | collective-permute-start | bytes 786440 | tf_op jit(solution)/shard_map/ppermute | solution.py:286
  53.2 2.3 %all-gather = bf16[8,128,256]{2,1,0:T(8,128)(2,1)S(1)} all-gather(bf16[4,128,256]{2,1,0:T(8,128)(2,1)S(1)} %collective-permute-done.6), channel_id=2, replica_groups=mesh['x'=4,'yh'=4,'c'=2,'yl'=2,'z'=12] {'c'}, dimensions={0}, use_global_device_ids=true | all-gather | bytes 786432 | tf_op jit(solution)/shard_map/all_gather | solution.py:287
  55.5 4.4 %shard_map.73 = (bf16[128,1024]{1,0:T(8,128)(2,1)S(1)}, bf16[4608,128]{1,0:T(8,128)(2,1)S(1)}, bf16[144,4608]{1,0:T(8,128)(2,1)S(1)}) custom-call(s32[9]{0:T(128)S(1)} %broadcast_minimum_fusion.scalars, bf16[128,1024]{1,0:T(8,128)(2,1)S(1)} %collective-permute-done.refs_0_, bf16[4,128,256]{2,1,0:T(8,128)(2,1)S(1)} %all_to_all.5.refs_1_, ...), custom_call_target="tpu_custom_call" | custom-call | tf_op jit(solution)/shard_map/pallas_call | solution.py:307
  59.9 3.7 %shard_map.76 = bf16[128,1024]{1,0:T(8,128)(2,1)S(1)} custom-call(s32[9]{0:T(128)S(1)} %broadcast_minimum_fusion.scalars, bf16[128,1024]{1,0:T(8,128)(2,1)S(1)} %collective-permute-done.10.refs_0_, bf16[4608,128]{1,0:T(8,128)(2,1)S(1)} %get-tuple-element.14.refs_1_, bf16[144,4608]{1,0:T(8,128)(2,1)S(1)} %get-tuple-element.15.refs_2_), custom_call_target="tpu_custom_call" | custom-call | tf_op jit(solution)/shard_map/pallas_call | solution.py:317
  63.7 3.9 %collective-permute-start.11 = (bf16[128,1024]{1,0:T(8,128)(2,1)S(1)}, bf16[128,1024]{1,0:T(8,128)(2,1)S(1)}, u32[]{:S(2)}, u32[]{:S(2)}) collective-permute-start(bf16[128,1024]{1,0:T(8,128)(2,1)S(1)} %shard_map.76), channel_id=1, source_target_pairs={{0,577},{1,578},{2,579},{3,580},{4,581},{5,582},{6,583},{7,584},{8... | collective-permute-start | bytes 786440 | tf_op jit(solution)/shard_map/ppermute | solution.py:326
  67.6 4.0 %collective-permute-start.12 = (bf16[128,1024]{1,0:T(8,128)(2,1)S(1)}, bf16[128,1024]{1,0:T(8,128)(2,1)S(1)}, u32[]{:S(2)}, u32[]{:S(2)}) collective-permute-start(bf16[128,1024]{1,0:T(8,128)(2,1)S(1)} %get-tuple-element.18), channel_id=1, source_target_pairs={{0,385},{1,386},{2,387},{3,388},{4,389},{5,390},{6,391},{7,392},{8... | collective-permute-start | bytes 786440 | tf_op jit(solution)/shard_map/ppermute | solution.py:326
  71.6 2.5 %shard_map.75 = bf16[128,1024]{1,0:T(8,128)(2,1)S(1)} custom-call(s32[9]{0:T(128)S(1)} %broadcast_minimum_fusion.scalars, bf16[128,1024]{1,0:T(8,128)(2,1)S(1)} %collective-permute-done.8.refs_0_, bf16[4608,128]{1,0:T(8,128)(2,1)S(1)} %get-tuple-element.14.refs_1_, bf16[144,4608]{1,0:T(8,128)(2,1)S(1)} %get-tuple-element.15.refs_2_), custom_call_target="tpu_custom_call" | custom-call | tf_op jit(solution)/shard_map/pallas_call | solution.py:317
  74.0 5.9 %collective-permute-start.9 = (bf16[128,1024]{1,0:T(8,128)(2,1)S(1)}, bf16[128,1024]{1,0:T(8,128)(2,1)S(1)}, u32[]{:S(2)}, u32[]{:S(2)}) collective-permute-start(bf16[128,1024]{1,0:T(8,128)(2,1)S(1)} %shard_map.75), channel_id=1, source_target_pairs={{0,193},{1,194},{2,195},{3,196},{4,197},{5,198},{6,199},{7,200},{8... | collective-permute-start | bytes 786440 | tf_op jit(solution)/shard_map/ppermute | solution.py:326
  79.9 2.5 %shard_map.74 = bf16[128,1024]{1,0:T(8,128)(2,1)S(1)} custom-call(s32[9]{0:T(128)S(1)} %broadcast_minimum_fusion.scalars, bf16[128,1024]{1,0:T(8,128)(2,1)S(1)} %get-tuple-element.12.refs_0_, bf16[4608,128]{1,0:T(8,128)(2,1)S(1)} %get-tuple-element.14.refs_1_, bf16[144,4608]{1,0:T(8,128)(2,1)S(1)} %get-tuple-element.15.refs_2_), custom_call_target="tpu_custom_call" | custom-call | tf_op jit(solution)/shard_map/pallas_call | solution.py:317
  82.4 4.6 %collective-permute-start.7 = (bf16[128,1024]{1,0:T(8,128)(2,1)S(1)}, bf16[128,1024]{1,0:T(8,128)(2,1)S(1)}, u32[]{:S(2)}, u32[]{:S(2)}) collective-permute-start(bf16[128,1024]{1,0:T(8,128)(2,1)S(1)} %shard_map.74), channel_id=1, source_target_pairs={{0,1},{1,2},{2,3},{3,4},{4,5},{5,6},{6,7},{7,8},{8,9},{9,10},{10,1... | collective-permute-start | bytes 786440 | tf_op jit(solution)/shard_map/ppermute | solution.py:326
  89.1 5.2 %collective-permute-done.9.piece_ref = bf16[128,1024]{1,0:T(8,128)(2,1)S(1)} collective-permute-done((bf16[128,1024]{1,0:T(8,128)(2,1)S(1)}, bf16[128,1024]{1,0:T(8,128)(2,1)S(1)}, u32[]{:S(2)}, u32[]{:S(2)}) %collective-permute-start.9) | collective-permute-done | bytes 262176 | tf_op jit(solution)/shard_map/ppermute | solution.py:326
  95.0 5.8 %collective-permute-done.7.piece_ref = bf16[128,1024]{1,0:T(8,128)(2,1)S(1)} collective-permute-done((bf16[128,1024]{1,0:T(8,128)(2,1)S(1)}, bf16[128,1024]{1,0:T(8,128)(2,1)S(1)}, u32[]{:S(2)}, u32[]{:S(2)}) %collective-permute-start.7) | collective-permute-done | bytes 262176 | tf_op jit(solution)/shard_map/ppermute | solution.py:326
  (18 shorter events, 3.3 us)
Async XLA Ops:
  0.0 34.6 %copy-start = (bf16[1,128,4096]{2,1,0:T(8,128)(2,1)S(1)}, bf16[1,128,4096]{2,1,0:T(8,128)(2,1)}, u32[]{:S(2)}) copy-start(bf16[1,128,4096]{2,1,0:T(8,128)(2,1)} %param.7) | copy-start | bytes 3145732
  12.9 13.2 %collective-permute-start.2 = (bf16[4,128,256]{2,1,0:T(8,128)(2,1)S(1)}, bf16[4,128,256]{2,1,0:T(8,128)(2,1)S(1)}, u32[]{:S(2)}, u32[]{:S(2)}) collective-permute-start(bf16[4,128,256]{2,1,0:T(8,128)(2,1)S(1)} %all_to_all.5.refs_1_), channel_id=1, source_target_pairs={{0,48},{24,168},{48,96},{72,24},{96,144},{120,72},{144,0},{168,120... | collective-permute-start | bytes 786440 | tf_op jit(solution)/shard_map/ppermute | solution.py:281
  18.8 13.1 %collective-permute-start.1 = (bf16[4,128,256]{2,1,0:T(8,128)(2,1)S(1)}, bf16[4,128,256]{2,1,0:T(8,128)(2,1)S(1)}, u32[]{:S(2)}, u32[]{:S(2)}) collective-permute-start(bf16[4,128,256]{2,1,0:T(8,128)(2,1)S(1)} %all_to_all.5.refs_1_), channel_id=1, source_target_pairs={{0,24},{24,0},{1,25},{25,1},{2,26},{26,2},{3,27},{27,3},{4,28},{28... | collective-permute-start | bytes 786440 | tf_op jit(solution)/shard_map/ppermute | solution.py:282
  26.1 19.1 %collective-permute-start.6 = (bf16[4,128,256]{2,1,0:T(8,128)(2,1)S(1)}, bf16[4,128,256]{2,1,0:T(8,128)(2,1)S(1)}, u32[]{:S(2)}, u32[]{:S(2)}) collective-permute-start(bf16[4,128,256]{2,1,0:T(8,128)(2,1)S(1)} %collective-permute-done.2.refs_3_), channel_id=1, source_target_pairs={{0,48},{24,168},{48,96},{72,24},{96,144},{120,72},{144,0},{168,120... | collective-permute-start | bytes 786440 | tf_op jit(solution)/shard_map/ppermute | solution.py:284
  31.9 19.3 %collective-permute-start.3 = (bf16[4,128,256]{2,1,0:T(8,128)(2,1)S(1)}, bf16[4,128,256]{2,1,0:T(8,128)(2,1)S(1)}, u32[]{:S(2)}, u32[]{:S(2)}) collective-permute-start(bf16[4,128,256]{2,1,0:T(8,128)(2,1)S(1)} %collective-permute-done.1.refs_2_), channel_id=1, source_target_pairs={{0,48},{24,168},{48,96},{72,24},{96,144},{120,72},{144,0},{168,120... | collective-permute-start | bytes 786440 | tf_op jit(solution)/shard_map/ppermute | solution.py:283
  36.1 19.3 %collective-permute-start = (bf16[128,1024]{1,0:T(8,128)(2,1)S(1)}, bf16[128,1024]{1,0:T(8,128)(2,1)S(1)}, u32[]{:S(2)}, u32[]{:S(2)}) collective-permute-start(bf16[128,1024]{1,0:T(8,128)(2,1)S(1)} %get-tuple-element.13), channel_id=1, source_target_pairs={{0,384},{1,385},{2,386},{3,387},{4,388},{5,389},{6,390},{7,391},{8... | collective-permute-start | bytes 786440 | tf_op jit(solution)/shard_map/ppermute | solution.py:291
  38.7 21.2 %collective-permute-start.10 = (bf16[128,1024]{1,0:T(8,128)(2,1)S(1)}, bf16[128,1024]{1,0:T(8,128)(2,1)S(1)}, u32[]{:S(2)}, u32[]{:S(2)}) collective-permute-start(bf16[128,1024]{1,0:T(8,128)(2,1)S(1)} %get-tuple-element.17), channel_id=1, source_target_pairs={{0,192},{1,193},{2,194},{3,195},{4,196},{5,197},{6,198},{7,199},{8... | collective-permute-start | bytes 786440 | tf_op jit(solution)/shard_map/ppermute | solution.py:291
  41.4 30.1 %collective-permute-start.8 = (bf16[128,1024]{1,0:T(8,128)(2,1)S(1)}, bf16[128,1024]{1,0:T(8,128)(2,1)S(1)}, u32[]{:S(2)}, u32[]{:S(2)}) collective-permute-start(bf16[128,1024]{1,0:T(8,128)(2,1)S(1)} %get-tuple-element.16), channel_id=1, source_target_pairs={{0,576},{1,577},{2,578},{3,579},{4,580},{5,581},{6,582},{7,583},{8... | collective-permute-start | bytes 786440 | tf_op jit(solution)/shard_map/ppermute | solution.py:291
  45.2 10.2 %collective-permute-start.5 = (bf16[4,128,256]{2,1,0:T(8,128)(2,1)S(1)}, bf16[4,128,256]{2,1,0:T(8,128)(2,1)S(1)}, u32[]{:S(2)}, u32[]{:S(2)}) collective-permute-start(bf16[4,128,256]{2,1,0:T(8,128)(2,1)S(1)} %collective-permute-done.2.refs_3_), channel_id=1, source_target_pairs={{0,24},{24,0},{1,25},{25,1},{2,26},{26,2},{3,27},{27,3},{4,28},{28... | collective-permute-start | bytes 786440 | tf_op jit(solution)/shard_map/ppermute | solution.py:285
  51.2 4.3 %collective-permute-start.4 = (bf16[4,128,256]{2,1,0:T(8,128)(2,1)S(1)}, bf16[4,128,256]{2,1,0:T(8,128)(2,1)S(1)}, u32[]{:S(2)}, u32[]{:S(2)}) collective-permute-start(bf16[4,128,256]{2,1,0:T(8,128)(2,1)S(1)} %collective-permute-done.3.refs_4_), channel_id=1, source_target_pairs={{0,24},{24,0},{1,25},{25,1},{2,26},{26,2},{3,27},{27,3},{4,28},{28... | collective-permute-start | bytes 786440 | tf_op jit(solution)/shard_map/ppermute | solution.py:286
  63.7 24.7 %collective-permute-start.11 = (bf16[128,1024]{1,0:T(8,128)(2,1)S(1)}, bf16[128,1024]{1,0:T(8,128)(2,1)S(1)}, u32[]{:S(2)}, u32[]{:S(2)}) collective-permute-start(bf16[128,1024]{1,0:T(8,128)(2,1)S(1)} %shard_map.76), channel_id=1, source_target_pairs={{0,577},{1,578},{2,579},{3,580},{4,581},{5,582},{6,583},{7,584},{8... | collective-permute-start | bytes 786440 | tf_op jit(solution)/shard_map/ppermute | solution.py:326
  67.6 20.1 %collective-permute-start.12 = (bf16[128,1024]{1,0:T(8,128)(2,1)S(1)}, bf16[128,1024]{1,0:T(8,128)(2,1)S(1)}, u32[]{:S(2)}, u32[]{:S(2)}) collective-permute-start(bf16[128,1024]{1,0:T(8,128)(2,1)S(1)} %get-tuple-element.18), channel_id=1, source_target_pairs={{0,385},{1,386},{2,387},{3,388},{4,389},{5,390},{6,391},{7,392},{8... | collective-permute-start | bytes 786440 | tf_op jit(solution)/shard_map/ppermute | solution.py:326
  74.0 20.2 %collective-permute-start.9 = (bf16[128,1024]{1,0:T(8,128)(2,1)S(1)}, bf16[128,1024]{1,0:T(8,128)(2,1)S(1)}, u32[]{:S(2)}, u32[]{:S(2)}) collective-permute-start(bf16[128,1024]{1,0:T(8,128)(2,1)S(1)} %shard_map.75), channel_id=1, source_target_pairs={{0,193},{1,194},{2,195},{3,196},{4,197},{5,198},{6,199},{7,200},{8... | collective-permute-start | bytes 786440 | tf_op jit(solution)/shard_map/ppermute | solution.py:326
  82.4 18.4 %collective-permute-start.7 = (bf16[128,1024]{1,0:T(8,128)(2,1)S(1)}, bf16[128,1024]{1,0:T(8,128)(2,1)S(1)}, u32[]{:S(2)}, u32[]{:S(2)}) collective-permute-start(bf16[128,1024]{1,0:T(8,128)(2,1)S(1)} %shard_map.74), channel_id=1, source_target_pairs={{0,1},{1,2},{2,3},{3,4},{4,5},{5,6},{6,7},{7,8},{8,9},{9,10},{10,1... | collective-permute-start | bytes 786440 | tf_op jit(solution)/shard_map/ppermute | solution.py:326
